TPU v7x, 256 devices: a whole 4x4x8 slice. The times are simulated.
256 devices in a mesh: phase: 8 (over y, core), seg: 32 (over z, x).
Axes of the slice: x: 4, y: 4, z: 8, core: 2. Of those that a mesh axis runs over, the one named last changes fastest.
Arguments:
- stream: bfloat16 [2, 4096, 4096], P(None, 'seg'), may hold values from -6 to 6
- doc_ids: int32 [2, 4096], P(None, 'seg'), may hold values from 0 to 7, never falling along the last dimension, each value on 1 to 2048 neighbouring positions
- in_proj: bfloat16 [8, 4096, 576], P('phase'), may hold values from -0.09375 to 0.09375
- conv_weight: float32 [8, 4, 4096], P('phase'), may hold values from -3 to 3
- conv_bias: float32 [8, 4096], P('phase'), may hold values from -3 to 3
- decay_log: float32 [8, 64], P('phase'), may hold values from -6.3 to 0.7
- step_bias: float32 [8, 64], P('phase'), may hold values from -4.5 to -2.5
- skip_gain: float32 [8, 64], P('phase'), may hold values from 0.5 to 1.5
- norm_gain: float32 [8, 4096], P('phase'), may hold values from 0.1 to 1.9
Outputs:
- layer_out: bfloat16 [8, 2, 4096, 4096], P('phase', None, 'seg')
Inputs may be any that keep to these rules, and one draw needn't show every extreme that they name: `doc_ids`: ids never fall along a stream.
All inputs are finite; a program needn't handle non-finite values.
Results may differ from a plain program's by a relative error of at most 0.033.
Values may be sent and summed in bfloat16 or wider, within the bound.
A program may use at most 64 MiB of HBM per device.

v0:
```python
import jax
import jax.numpy as jnp
from jax import lax
from jax.sharding import PartitionSpec as P

HEADS = 64
HEAD_DIM = 64
STATE = 64
GROUPS = 4
KERNEL = 4
MICRO = 2


def from_behind(value, axis, steps):
    count = lax.axis_size(axis)
    initial, last = (max(0, -steps), min(count, count - steps))
    return lax.ppermute(value, axis, [(source, source + steps) for source in range(initial, last)])


def product(form, left, right):
    return jnp.einsum(form, left, right, preferred_element_type=jnp.float32)


def conv_mix(padded, padded_ids, token_ids, conv_weight, conv_bias):
    length = token_ids.shape[0]
    summed = jnp.zeros((length, padded.shape[1]), jnp.float32)
    for offset in range(KERNEL):
        shifted = padded[offset : offset + length].astype(jnp.float32)
        same_doc = padded_ids[offset : offset + length] == token_ids
        summed = summed + conv_weight[offset][None, :] * jnp.where(same_doc[:, None], shifted, 0.0)
    return jax.nn.silu(summed + conv_bias[None, :]).astype(jnp.bfloat16)


def project(tokens, in_proj, step_bias):
    projected = jnp.dot(tokens, in_proj, preferred_element_type=jnp.float32)
    bc_width = GROUPS * STATE
    b_rows = projected[:, :bc_width].reshape(-1, GROUPS, STATE).astype(jnp.bfloat16)
    c_rows = projected[:, bc_width : 2 * bc_width].reshape(-1, GROUPS, STATE).astype(jnp.bfloat16)
    step_size = jax.nn.softplus(projected[:, 2 * bc_width :] + step_bias[None, :])
    return (b_rows, c_rows, step_size)


def block_terms(inputs, b_rows, c_rows, step_size, log_decay, block_ids, prior_id):
    length = inputs.shape[0]
    per_group = HEADS // GROUPS
    running = jnp.cumsum(log_decay, axis=0)
    places = jnp.arange(length)
    inside = (block_ids[:, None] == block_ids[None, :]) & (places[:, None] >= places[None, :])
    decays = jnp.where(
        inside[:, :, None],
        jnp.exp(jnp.minimum(running[:, None, :] - running[None, :, :], 0.0)),
        0.0,
    )
    scores = product("tgn,sgn->tsg", c_rows, b_rows)
    weights = (
        scores[:, :, :, None]
        * (decays * step_size[None, :, :]).reshape(length, length, GROUPS, per_group)
    ).astype(jnp.bfloat16)
    grouped = inputs.reshape(length, GROUPS, per_group, HEAD_DIM)
    intra_part = product("tsgj,sgjp->tgjp", weights, grouped).reshape(length, HEADS, HEAD_DIM)
    carry_gain = jnp.where((block_ids == prior_id)[:, None], jnp.exp(running), 0.0)
    tail_weight = (
        jnp.where(
            (block_ids == block_ids[-1])[:, None], jnp.exp(running[-1][None, :] - running), 0.0
        )
        * step_size
    )
    scaled = (
        tail_weight.reshape(length, GROUPS, per_group)[:, :, :, None] * grouped.astype(jnp.float32)
    ).astype(jnp.bfloat16)
    local_state = product("sgjp,sgn->gjpn", scaled, b_rows).reshape(HEADS, HEAD_DIM, STATE)
    return (intra_part, carry_gain, local_state, carry_gain[-1])


def carry_term(c_rows, carried, carry_gain):
    length = c_rows.shape[0]
    per_group = HEADS // GROUPS
    grouped = carried.astype(jnp.bfloat16).reshape(GROUPS, per_group, HEAD_DIM, STATE)
    carry_part = product("tgn,gjpn->tgjp", c_rows, grouped).reshape(length, HEADS, HEAD_DIM)
    return carry_part * carry_gain[:, :, None]


def finish(tokens, mixed_out, norm_gain):
    flat_mixed = mixed_out.reshape(tokens.shape[0], -1)
    inverse_rms = lax.rsqrt(jnp.mean(flat_mixed * flat_mixed, axis=1, keepdims=True) + 1e-05)
    return (tokens.astype(jnp.float32) + norm_gain[None, :] * flat_mixed * inverse_rms).astype(
        jnp.bfloat16
    )


def joined(early, later):
    return (early[0] * later[0], later[0] * early[1] + later[1])


def carry_state(local_state, end_gain):
    flat_state = local_state.reshape(HEADS, HEAD_DIM * STATE)
    gains = end_gain.reshape(HEADS, 1)
    moved = (
        lax.all_to_all(gains[None], "seg", split_axis=1, concat_axis=0, tiled=True),
        lax.all_to_all(flat_state[None], "seg", split_axis=1, concat_axis=0, tiled=True),
    )
    running = lax.associative_scan(joined, moved, axis=0)
    entering = jnp.concatenate([jnp.zeros_like(running[1][:1]), running[1][:-1]], axis=0)
    returned = lax.all_to_all(
        entering.astype(jnp.bfloat16), "seg", split_axis=0, concat_axis=1, tiled=True
    ).astype(entering.dtype)
    return returned.reshape(HEADS, HEAD_DIM, STATE)


def local_layer(
    tokens,
    token_ids,
    before,
    in_proj,
    conv_weight,
    conv_bias,
    decay_log,
    step_bias,
    skip_gain,
    norm_gain,
):
    length = tokens.shape[0]
    margin = KERNEL - 1
    shifted = from_behind(tokens[length - margin :], "seg", 1)
    b_rows, c_rows, step_size = project(tokens, in_proj, step_bias)
    padded = jnp.concatenate([shifted, tokens], axis=0)
    padded_ids = jnp.concatenate([before, token_ids], axis=0)
    inputs = conv_mix(padded, padded_ids, token_ids, conv_weight, conv_bias).reshape(
        length, HEADS, HEAD_DIM
    )
    log_decay = -jnp.exp(decay_log)[None, :] * step_size
    intra_part, carry_gain, local_state, end_gain = block_terms(
        inputs, b_rows, c_rows, step_size, log_decay, token_ids, before[margin - 1]
    )
    carried = carry_state(local_state, end_gain)
    mixed_out = (
        intra_part
        + carry_term(c_rows, carried, carry_gain)
        + skip_gain[None, :, None] * inputs.astype(jnp.float32)
    )
    return finish(tokens, mixed_out, norm_gain)


def body(
    stream, doc_ids, in_proj, conv_weight, conv_bias, decay_log, step_bias, skip_gain, norm_gain
):
    phase_index = lax.axis_index("phase")
    phase_count = lax.axis_size("phase")
    margin = KERNEL - 1
    length = doc_ids.shape[1]
    edge_ids = from_behind(doc_ids[:, length - margin :] + 1, "seg", 1) - 1
    params = (
        in_proj[0],
        conv_weight[0],
        conv_bias[0],
        decay_log[0],
        step_bias[0],
        skip_gain[0],
        norm_gain[0],
    )

    def advance(time_step, loop_carry):
        received, layer_out = loop_carry
        batch_index = time_step - phase_index
        is_valid = (batch_index >= 0) & (batch_index < MICRO)
        picked = jnp.clip(batch_index, 0, MICRO - 1)
        first_input = lax.dynamic_index_in_dim(stream, picked, 0, keepdims=False)
        tokens = jnp.where(phase_index == 0, first_input, received)
        token_ids = lax.dynamic_index_in_dim(doc_ids, picked, 0, keepdims=False)
        before = lax.dynamic_index_in_dim(edge_ids, picked, 0, keepdims=False)
        result = local_layer(tokens, token_ids, before, *params)
        previous = lax.dynamic_index_in_dim(layer_out, picked, 0, keepdims=False)
        layer_out = lax.dynamic_update_index_in_dim(
            layer_out, jnp.where(is_valid, result, previous), picked, 0
        )
        received = from_behind(result, "phase", 1)
        return (received, layer_out)

    initial = (jnp.zeros(stream.shape[1:], jnp.bfloat16), jnp.zeros(stream.shape, jnp.bfloat16))
    final_carry = lax.fori_loop(0, MICRO + phase_count - 1, advance, initial)
    return final_carry[1][None]


def solution(mesh):
    placed = (
        P(None, "seg", None),
        P(None, "seg"),
        P("phase", None, None),
        P("phase", None, None),
        P("phase", None),
        P("phase", None),
        P("phase", None),
        P("phase", None),
        P("phase", None),
    )
    return jax.shard_map(
        body, mesh=mesh, in_specs=placed, out_specs=P("phase", None, "seg", None), check_vma=False
    )
```

profile of v0, /device:TPU:1, one launch (start us, length us, event | category | flops | bytes accessed | tf_op | source)
XLA Modules:
  0.0 1543.8 jit_solution(11858744918664756777)
XLA Ops:
  14.1 1529.7 %while.17 = (s32[]{:T(128)}, bf16[128,4096]{0,1:T(8,128)(2,1)S(1)}, bf16[2,128,4096]{2,1,0:T(8,128)(2,1)}, pred[]{:T(512)}, s32[]{:T(128)}, /*index=5*/bf16[2,12...) while((s32[]{:T(128)}, bf16[128,4096]{0,1:T(8,128)(2,1)S(1)}, ...), condition=%wide.region_3.4_spmd, body=%wide.region_0.3_spmd.sunk | while | flops 917242752 | bytes 103021864 | solution.py:180
  29.8 10.3 all-to-all-start.1
  52.8 9.1 all-to-all-start
  65.8 21.4 %all-to-all-done = f32[1,64,4096]{2,0,1:T(1,128)S(1)} async-done(((f32[1,64,4096]{2,0,1:T(1,128)}), f32[1,64,4096]{2,0,1:T(1,128)S(1)}, u32[]{:S(2)}, u32[]{:S(2)}) %all-to-all-start) | async-done | bytes 1048608 | tf_op jit(solution)/shard_map/while/body/eval_jaxpr/all_to_all | solution.py:100
  185.9 9.4 collective-permute-done.1
  228.6 9.1 all-to-all-start
  241.7 14.9 all-to-all-done
  341.8 17.3 %collective-permute-start.1 = (bf16[128,4096]{0,1:T(8,128)(2,1)}, bf16[128,4096]{0,1:T(8,128)(2,1)S(1)}, u32[]{:S(2)}, u32[]{:S(2)}) collective-permute-start(bf16[128,4096]{0,1:T(8,128)(2,1)} %get-tuple-element.566), channel_id=1, source_target_pairs={{0,32},{32,64},{64,96},{96,128},{128,160},{160,192},{192,224},{1,3... | collective-permute-start | bytes 3145736 | tf_op jit(solution)/shard_map/while/body/eval_jaxpr/ppermute | solution.py:17
  361.7 9.4 collective-permute-done.1
  404.4 9.1 all-to-all-start
  417.5 13.3 all-to-all-done
  515.9 18.3 %collective-permute-start.1 = (bf16[128,4096]{0,1:T(8,128)(2,1)}, bf16[128,4096]{0,1:T(8,128)(2,1)S(1)}, u32[]{:S(2)}, u32[]{:S(2)}) collective-permute-start(bf16[128,4096]{0,1:T(8,128)(2,1)} %get-tuple-element.566), channel_id=1, source_target_pairs={{0,32},{32,64},{64,96},{96,128},{128,160},{160,192},{192,224},{1,3... | collective-permute-start | bytes 3145736 | tf_op jit(solution)/shard_map/while/body/eval_jaxpr/ppermute | solution.py:17
  536.8 9.4 collective-permute-done.1
  579.6 9.1 all-to-all-start
  592.6 13.3 all-to-all-done
  691.0 11.3 collective-permute-start.1
  704.9 9.4 collective-permute-done.1
  748.7 9.1 all-to-all-start
  761.8 13.3 all-to-all-done
  870.8 9.4 collective-permute-done.1
  914.6 9.1 all-to-all-start
  927.7 13.3 all-to-all-done
  1036.7 9.4 collective-permute-done.1
  1080.5 9.1 all-to-all-start
  1093.5 13.3 all-to-all-done
  1202.6 9.4 collective-permute-done.1
  1246.4 9.1 all-to-all-start
  1259.4 13.3 all-to-all-done
  1368.4 9.4 collective-permute-done.1
  1412.3 9.1 all-to-all-start
  1425.3 13.3 all-to-all-done
  1534.3 9.4 collective-permute-done.1
  (1315 shorter events, 1185.4 us)
Async XLA Ops:
  17.0 23.9 %collective-permute-start = (bf16[3,4096]{1,0:T(4,128)(2,1)S(1)}, bf16[3,4096]{1,0:T(4,128)(2,1)S(1)}, u32[]{:S(2)}, u32[]{:S(2)}) collective-permute-start(bf16[3,4096]{1,0:T(4,128)(2,1)S(1)} %copy.127), channel_id=1, source_target_pairs={{0,1},{1,2},{2,3},{3,4},{4,5},{5,6},{6,7},{7,8},{8,9},{9,10},{10,1... | collective-permute-start | bytes 73736 | tf_op jit(solution)/shard_map/while/body/eval_jaxpr/ppermute | solution.py:17
  29.8 22.9 %all-to-all-start.1 = ((f32[1,64,1]{2,0,1:T(1,128)}), f32[1,64,1]{2,0,1:T(1,128)}, u32[]{:S(2)}, u32[]{:S(2)}) async-start(f32[1,64,1]{2,0,1:T(1,128)} %bitcast.189), calls=%async_computation.1 | async-start | bytes 65536 | tf_op jit(solution)/shard_map/while/body/eval_jaxpr/all_to_all | solution.py:99
  52.8 34.4 %all-to-all-start = ((f32[1,64,4096]{2,0,1:T(1,128)}), f32[1,64,4096]{2,0,1:T(1,128)S(1)}, u32[]{:S(2)}, u32[]{:S(2)}) async-start(f32[1,64,4096]{2,0,1:T(1,128)} %reshape.270), calls=%async_computation | async-start | bytes 2097152 | tf_op jit(solution)/shard_map/while/body/eval_jaxpr/all_to_all | solution.py:100
  145.8 21.6 %all-to-all-start.2 = ((bf16[32,2,4096]{2,1,0:T(2,128)(2,1)}), bf16[32,2,4096]{2,1,0:T(2,128)(2,1)}, u32[]{:S(2)}, u32[]{:S(2)}) async-start(bf16[32,2,4096]{2,1,0:T(2,128)(2,1)} %concatenate.60), calls=%async_computation.2 | async-start | bytes 1048576 | tf_op jit(solution)/shard_map/while/body/eval_jaxpr/all_to_all | solution.py:104
  175.9 19.4 %collective-permute-start.1 = (bf16[128,4096]{0,1:T(8,128)(2,1)}, bf16[128,4096]{0,1:T(8,128)(2,1)S(1)}, u32[]{:S(2)}, u32[]{:S(2)}) collective-permute-start(bf16[128,4096]{0,1:T(8,128)(2,1)} %get-tuple-element.566), channel_id=1, source_target_pairs={{0,32},{32,64},{64,96},{96,128},{128,160},{160,192},{192,224},{1,3... | collective-permute-start | bytes 3145736 | tf_op jit(solution)/shard_map/while/body/eval_jaxpr/ppermute | solution.py:17
  198.2 18.6 %collective-permute-start = (bf16[3,4096]{1,0:T(4,128)(2,1)S(1)}, bf16[3,4096]{1,0:T(4,128)(2,1)S(1)}, u32[]{:S(2)}, u32[]{:S(2)}) collective-permute-start(bf16[3,4096]{1,0:T(4,128)(2,1)S(1)} %copy.127), channel_id=1, source_target_pairs={{0,1},{1,2},{2,3},{3,4},{4,5},{5,6},{6,7},{7,8},{8,9},{9,10},{10,1... | collective-permute-start | bytes 73736 | tf_op jit(solution)/shard_map/while/body/eval_jaxpr/ppermute | solution.py:17
  228.6 28.0 %all-to-all-start = ((f32[1,64,4096]{2,0,1:T(1,128)}), f32[1,64,4096]{2,0,1:T(1,128)S(1)}, u32[]{:S(2)}, u32[]{:S(2)}) async-start(f32[1,64,4096]{2,0,1:T(1,128)} %reshape.270), calls=%async_computation | async-start | bytes 2097152 | tf_op jit(solution)/shard_map/while/body/eval_jaxpr/all_to_all | solution.py:100
  341.8 29.4 %collective-permute-start.1 = (bf16[128,4096]{0,1:T(8,128)(2,1)}, bf16[128,4096]{0,1:T(8,128)(2,1)S(1)}, u32[]{:S(2)}, u32[]{:S(2)}) collective-permute-start(bf16[128,4096]{0,1:T(8,128)(2,1)} %get-tuple-element.566), channel_id=1, source_target_pairs={{0,32},{32,64},{64,96},{96,128},{128,160},{160,192},{192,224},{1,3... | collective-permute-start | bytes 3145736 | tf_op jit(solution)/shard_map/while/body/eval_jaxpr/ppermute | solution.py:17
  404.4 26.3 %all-to-all-start = ((f32[1,64,4096]{2,0,1:T(1,128)}), f32[1,64,4096]{2,0,1:T(1,128)S(1)}, u32[]{:S(2)}, u32[]{:S(2)}) async-start(f32[1,64,4096]{2,0,1:T(1,128)} %reshape.270), calls=%async_computation | async-start | bytes 2097152 | tf_op jit(solution)/shard_map/while/body/eval_jaxpr/all_to_all | solution.py:100
  515.9 30.3 %collective-permute-start.1 = (bf16[128,4096]{0,1:T(8,128)(2,1)}, bf16[128,4096]{0,1:T(8,128)(2,1)S(1)}, u32[]{:S(2)}, u32[]{:S(2)}) collective-permute-start(bf16[128,4096]{0,1:T(8,128)(2,1)} %get-tuple-element.566), channel_id=1, source_target_pairs={{0,32},{32,64},{64,96},{96,128},{128,160},{160,192},{192,224},{1,3... | collective-permute-start | bytes 3145736 | tf_op jit(solution)/shard_map/while/body/eval_jaxpr/ppermute | solution.py:17
  579.6 26.3 %all-to-all-start = ((f32[1,64,4096]{2,0,1:T(1,128)}), f32[1,64,4096]{2,0,1:T(1,128)S(1)}, u32[]{:S(2)}, u32[]{:S(2)}) async-start(f32[1,64,4096]{2,0,1:T(1,128)} %reshape.270), calls=%async_computation | async-start | bytes 2097152 | tf_op jit(solution)/shard_map/while/body/eval_jaxpr/all_to_all | solution.py:100
  691.0 23.3 %collective-permute-start.1 = (bf16[128,4096]{0,1:T(8,128)(2,1)}, bf16[128,4096]{0,1:T(8,128)(2,1)S(1)}, u32[]{:S(2)}, u32[]{:S(2)}) collective-permute-start(bf16[128,4096]{0,1:T(8,128)(2,1)} %get-tuple-element.566), channel_id=1, source_target_pairs={{0,32},{32,64},{64,96},{96,128},{128,160},{160,192},{192,224},{1,3... | collective-permute-start | bytes 3145736 | tf_op jit(solution)/shard_map/while/body/eval_jaxpr/ppermute | solution.py:17
  717.2 19.6 %collective-permute-start = (bf16[3,4096]{1,0:T(4,128)(2,1)S(1)}, bf16[3,4096]{1,0:T(4,128)(2,1)S(1)}, u32[]{:S(2)}, u32[]{:S(2)}) collective-permute-start(bf16[3,4096]{1,0:T(4,128)(2,1)S(1)} %copy.127), channel_id=1, source_target_pairs={{0,1},{1,2},{2,3},{3,4},{4,5},{5,6},{6,7},{7,8},{8,9},{9,10},{10,1... | collective-permute-start | bytes 73736 | tf_op jit(solution)/shard_map/while/body/eval_jaxpr/ppermute | solution.py:17
  729.0 19.7 %all-to-all-start.1 = ((f32[1,64,1]{2,0,1:T(1,128)}), f32[1,64,1]{2,0,1:T(1,128)}, u32[]{:S(2)}, u32[]{:S(2)}) async-start(f32[1,64,1]{2,0,1:T(1,128)} %bitcast.189), calls=%async_computation.1 | async-start | bytes 65536 | tf_op jit(solution)/shard_map/while/body/eval_jaxpr/all_to_all | solution.py:99
  748.7 26.3 %all-to-all-start = ((f32[1,64,4096]{2,0,1:T(1,128)}), f32[1,64,4096]{2,0,1:T(1,128)S(1)}, u32[]{:S(2)}, u32[]{:S(2)}) async-start(f32[1,64,4096]{2,0,1:T(1,128)} %reshape.270), calls=%async_computation | async-start | bytes 2097152 | tf_op jit(solution)/shard_map/while/body/eval_jaxpr/all_to_all | solution.py:100
  860.2 20.0 %collective-permute-start.1 = (bf16[128,4096]{0,1:T(8,128)(2,1)}, bf16[128,4096]{0,1:T(8,128)(2,1)S(1)}, u32[]{:S(2)}, u32[]{:S(2)}) collective-permute-start(bf16[128,4096]{0,1:T(8,128)(2,1)} %get-tuple-element.566), channel_id=1, source_target_pairs={{0,32},{32,64},{64,96},{96,128},{128,160},{160,192},{192,224},{1,3... | collective-permute-start | bytes 3145736 | tf_op jit(solution)/shard_map/while/body/eval_jaxpr/ppermute | solution.py:17
  883.1 19.6 %collective-permute-start = (bf16[3,4096]{1,0:T(4,128)(2,1)S(1)}, bf16[3,4096]{1,0:T(4,128)(2,1)S(1)}, u32[]{:S(2)}, u32[]{:S(2)}) collective-permute-start(bf16[3,4096]{1,0:T(4,128)(2,1)S(1)} %copy.127), channel_id=1, source_target_pairs={{0,1},{1,2},{2,3},{3,4},{4,5},{5,6},{6,7},{7,8},{8,9},{9,10},{10,1... | collective-permute-start | bytes 73736 | tf_op jit(solution)/shard_map/while/body/eval_jaxpr/ppermute | solution.py:17
  895.1 19.5 %all-to-all-start.1 = ((f32[1,64,1]{2,0,1:T(1,128)}), f32[1,64,1]{2,0,1:T(1,128)}, u32[]{:S(2)}, u32[]{:S(2)}) async-start(f32[1,64,1]{2,0,1:T(1,128)} %bitcast.189), calls=%async_computation.1 | async-start | bytes 65536 | tf_op jit(solution)/shard_map/while/body/eval_jaxpr/all_to_all | solution.py:99
  914.6 26.3 %all-to-all-start = ((f32[1,64,4096]{2,0,1:T(1,128)}), f32[1,64,4096]{2,0,1:T(1,128)S(1)}, u32[]{:S(2)}, u32[]{:S(2)}) async-start(f32[1,64,4096]{2,0,1:T(1,128)} %reshape.270), calls=%async_computation | async-start | bytes 2097152 | tf_op jit(solution)/shard_map/while/body/eval_jaxpr/all_to_all | solution.py:100
  1026.1 20.0 %collective-permute-start.1 = (bf16[128,4096]{0,1:T(8,128)(2,1)}, bf16[128,4096]{0,1:T(8,128)(2,1)S(1)}, u32[]{:S(2)}, u32[]{:S(2)}) collective-permute-start(bf16[128,4096]{0,1:T(8,128)(2,1)} %get-tuple-element.566), channel_id=1, source_target_pairs={{0,32},{32,64},{64,96},{96,128},{128,160},{160,192},{192,224},{1,3... | collective-permute-start | bytes 3145736 | tf_op jit(solution)/shard_map/while/body/eval_jaxpr/ppermute | solution.py:17
  1049.0 19.6 %collective-permute-start = (bf16[3,4096]{1,0:T(4,128)(2,1)S(1)}, bf16[3,4096]{1,0:T(4,128)(2,1)S(1)}, u32[]{:S(2)}, u32[]{:S(2)}) collective-permute-start(bf16[3,4096]{1,0:T(4,128)(2,1)S(1)} %copy.127), channel_id=1, source_target_pairs={{0,1},{1,2},{2,3},{3,4},{4,5},{5,6},{6,7},{7,8},{8,9},{9,10},{10,1... | collective-permute-start | bytes 73736 | tf_op jit(solution)/shard_map/while/body/eval_jaxpr/ppermute | solution.py:17
  1061.0 19.5 %all-to-all-start.1 = ((f32[1,64,1]{2,0,1:T(1,128)}), f32[1,64,1]{2,0,1:T(1,128)}, u32[]{:S(2)}, u32[]{:S(2)}) async-start(f32[1,64,1]{2,0,1:T(1,128)} %bitcast.189), calls=%async_computation.1 | async-start | bytes 65536 | tf_op jit(solution)/shard_map/while/body/eval_jaxpr/all_to_all | solution.py:99
  1080.5 26.3 %all-to-all-start = ((f32[1,64,4096]{2,0,1:T(1,128)}), f32[1,64,4096]{2,0,1:T(1,128)S(1)}, u32[]{:S(2)}, u32[]{:S(2)}) async-start(f32[1,64,4096]{2,0,1:T(1,128)} %reshape.270), calls=%async_computation | async-start | bytes 2097152 | tf_op jit(solution)/shard_map/while/body/eval_jaxpr/all_to_all | solution.py:100
  1192.0 20.0 %collective-permute-start.1 = (bf16[128,4096]{0,1:T(8,128)(2,1)}, bf16[128,4096]{0,1:T(8,128)(2,1)S(1)}, u32[]{:S(2)}, u32[]{:S(2)}) collective-permute-start(bf16[128,4096]{0,1:T(8,128)(2,1)} %get-tuple-element.566), channel_id=1, source_target_pairs={{0,32},{32,64},{64,96},{96,128},{128,160},{160,192},{192,224},{1,3... | collective-permute-start | bytes 3145736 | tf_op jit(solution)/shard_map/while/body/eval_jaxpr/ppermute | solution.py:17
  1214.9 19.6 %collective-permute-start = (bf16[3,4096]{1,0:T(4,128)(2,1)S(1)}, bf16[3,4096]{1,0:T(4,128)(2,1)S(1)}, u32[]{:S(2)}, u32[]{:S(2)}) collective-permute-start(bf16[3,4096]{1,0:T(4,128)(2,1)S(1)} %copy.127), channel_id=1, source_target_pairs={{0,1},{1,2},{2,3},{3,4},{4,5},{5,6},{6,7},{7,8},{8,9},{9,10},{10,1... | collective-permute-start | bytes 73736 | tf_op jit(solution)/shard_map/while/body/eval_jaxpr/ppermute | solution.py:17
  1226.8 19.5 %all-to-all-start.1 = ((f32[1,64,1]{2,0,1:T(1,128)}), f32[1,64,1]{2,0,1:T(1,128)}, u32[]{:S(2)}, u32[]{:S(2)}) async-start(f32[1,64,1]{2,0,1:T(1,128)} %bitcast.189), calls=%async_computation.1 | async-start | bytes 65536 | tf_op jit(solution)/shard_map/while/body/eval_jaxpr/all_to_all | solution.py:99
  1246.4 26.3 %all-to-all-start = ((f32[1,64,4096]{2,0,1:T(1,128)}), f32[1,64,4096]{2,0,1:T(1,128)S(1)}, u32[]{:S(2)}, u32[]{:S(2)}) async-start(f32[1,64,4096]{2,0,1:T(1,128)} %reshape.270), calls=%async_computation | async-start | bytes 2097152 | tf_op jit(solution)/shard_map/while/body/eval_jaxpr/all_to_all | solution.py:100
  1357.8 20.0 %collective-permute-start.1 = (bf16[128,4096]{0,1:T(8,128)(2,1)}, bf16[128,4096]{0,1:T(8,128)(2,1)S(1)}, u32[]{:S(2)}, u32[]{:S(2)}) collective-permute-start(bf16[128,4096]{0,1:T(8,128)(2,1)} %get-tuple-element.566), channel_id=1, source_target_pairs={{0,32},{32,64},{64,96},{96,128},{128,160},{160,192},{192,224},{1,3... | collective-permute-start | bytes 3145736 | tf_op jit(solution)/shard_map/while/body/eval_jaxpr/ppermute | solution.py:17
  1380.8 19.6 %collective-permute-start = (bf16[3,4096]{1,0:T(4,128)(2,1)S(1)}, bf16[3,4096]{1,0:T(4,128)(2,1)S(1)}, u32[]{:S(2)}, u32[]{:S(2)}) collective-permute-start(bf16[3,4096]{1,0:T(4,128)(2,1)S(1)} %copy.127), channel_id=1, source_target_pairs={{0,1},{1,2},{2,3},{3,4},{4,5},{5,6},{6,7},{7,8},{8,9},{9,10},{10,1... | collective-permute-start | bytes 73736 | tf_op jit(solution)/shard_map/while/body/eval_jaxpr/ppermute | solution.py:17
  1392.7 19.5 %all-to-all-start.1 = ((f32[1,64,1]{2,0,1:T(1,128)}), f32[1,64,1]{2,0,1:T(1,128)}, u32[]{:S(2)}, u32[]{:S(2)}) async-start(f32[1,64,1]{2,0,1:T(1,128)} %bitcast.189), calls=%async_computation.1 | async-start | bytes 65536 | tf_op jit(solution)/shard_map/while/body/eval_jaxpr/all_to_all | solution.py:99
  1412.3 26.3 %all-to-all-start = ((f32[1,64,4096]{2,0,1:T(1,128)}), f32[1,64,4096]{2,0,1:T(1,128)S(1)}, u32[]{:S(2)}, u32[]{:S(2)}) async-start(f32[1,64,4096]{2,0,1:T(1,128)} %reshape.270), calls=%async_computation | async-start | bytes 2097152 | tf_op jit(solution)/shard_map/while/body/eval_jaxpr/all_to_all | solution.py:100
  1523.7 20.0 %collective-permute-start.1 = (bf16[128,4096]{0,1:T(8,128)(2,1)}, bf16[128,4096]{0,1:T(8,128)(2,1)S(1)}, u32[]{:S(2)}, u32[]{:S(2)}) collective-permute-start(bf16[128,4096]{0,1:T(8,128)(2,1)} %get-tuple-element.566), channel_id=1, source_target_pairs={{0,32},{32,64},{64,96},{96,128},{128,160},{160,192},{192,224},{1,3... | collective-permute-start | bytes 3145736 | tf_op jit(solution)/shard_map/while/body/eval_jaxpr/ppermute | solution.py:17
  (224 other events, 1952.5 us)
where the time goes:
time: 1570 us; the launch traced here: 1540 us
  local copies, waits for them, and re-layouts  557 us (35%)
  starting transfers between devices  314 us (20%)
  other arithmetic  311 us (20%)
  waiting for transfers between devices  234 us (15%)
  matrix products  123 us (8%)
    pad x54, local copies, waits for them, and re-layouts, carry_state(): running = lax.associative_scan(joined, moved, axis=0)  162 us
    all_to_all x9, waiting for transfers between devices, carry_state(): lax.all_to_all(flat_state[None], 'seg', split_axis=1, concat_axis=0, tile...  129 us
    ppermute x19, starting transfers between devices, from_behind(): lax.ppermute(value, axis, [(source, source + steps) for source in range(i...  119 us
    while x414, local copies, waits for them, and re-layouts  87.8 us
    ppermute x19, waiting for transfers between devices, from_behind(): lax.ppermute(value, axis, [(source, source + steps) for source in range(i...  84.8 us
    all_to_all x9, starting transfers between devices, carry_state(): lax.all_to_all(flat_state[None], 'seg', split_axis=1, concat_axis=0, tile...  82.3 us
    dot_general x36, matrix products, product(): return jnp.einsum(form, left, right, preferred_element_type=jnp.float32)  81.6 us
    all_to_all x9, starting transfers between devices, carry_state(): lax.all_to_all(gains[None], 'seg', split_axis=1, concat_axis=0, tiled=True)  62.8 us
  transfers between devices with their start and end apart: 46, of which 27 were waited for; matrix products, arithmetic and copies ran while one was open for 23% of the time, Pallas kernels for 0%

commit v1 on v0

v1 whole, which is shorter than its diff:
```python
import functools

import jax
import jax.numpy as jnp
from jax import lax
from jax.experimental import pallas as pl
from jax.experimental.pallas import tpu as pltpu
from jax.sharding import PartitionSpec as P

NY = 4
NC = 2
NX = 4
LAYERS = 8
HEADS = 64
HEAD_DIM = 64
STATE = 64
GROUPS = 4
KERNEL = 4
MICRO = 2
T = 128
CH = 1024
PER = 16
NCH = 8
REACH = 4
PROJ = 576
MESH = pl.DeviceIdType.MESH
F32 = jnp.float32
BF16 = jnp.bfloat16


def wait_bytes(ref, sem):
    pltpu.make_async_copy(ref, ref, sem).wait()


def kernel(
    nz,
    stream_ref,
    ids_ref,
    proj_ref,
    pp_ref,
    out_ref,
    wbuf,
    w0,
    strm,
    ubuf,
    gm,
    gmb,
    ppb,
    idsrc,
    idh,
    msk,
    halo,
    fbuf,
    inp,
    wts,
    bcu,
    bcm,
    bcuo,
    bcmo,
    su,
    sm,
    suo,
    smo,
    sg,
    lout,
    lrecv,
    gout,
    grecv,
    tout,
    ggout,
    trecv,
    ggrecv,
    rb,
    eout,
    ent,
    m0,
    gx,
    yr,
    ys,
    p0s,
    xr,
    xs,
    zr,
    zs,
    hr,
    hs,
    wr,
    wss,
    wrs,
    pps,
    outr,
    outs,
    idsem,
    loc,
):
    phase = lax.axis_index("phase")
    seg = lax.axis_index("seg")
    nseg = nz * NX
    y = phase // NC
    c = phase % NC
    z = seg // NX
    x = seg % NX

    def remote(src, dst, ssem, rsem, p, s):
        return pltpu.make_async_remote_copy(
            src_ref=src,
            dst_ref=dst,
            send_sem=ssem,
            recv_sem=rsem,
            device_id=(p, s),
            device_id_type=MESH,
        )

    barrier = pltpu.get_barrier_semaphore()
    count = 0
    for d in range(1, NY * NC):
        pl.semaphore_signal(barrier, inc=1, device_id=((phase + d) % (NY * NC), seg), device_id_type=MESH)
        count += 1
    for d in range(1, NX):
        pl.semaphore_signal(
            barrier, inc=1, device_id=(phase, z * NX + (x + d) % NX), device_id_type=MESH
        )
        count += 1
    for d in range(1, nz):
        pl.semaphore_signal(
            barrier, inc=1, device_id=(phase, ((z + d) % nz) * NX + x), device_id_type=MESH
        )
        count += 1
    for d in (1, nseg - 1):
        pl.semaphore_signal(barrier, inc=1, device_id=(phase, (seg + d) % nseg), device_id_type=MESH)
        count += 1

    cp_u = pltpu.make_async_copy(
        stream_ref.at[c, :, pl.ds(pl.multiple_of(y * CH, CH), CH)], ubuf.at[0], loc.at[0]
    )
    cp_u.start()
    cp_pp = pltpu.make_async_copy(pp_ref.at[y], ppb.at[phase], loc.at[1])
    cp_pp.start()

    @pl.when(phase == 0)
    def _():
        for k in range(4):
            pltpu.make_async_copy(proj_ref.at[0, pl.ds(k * CH, CH), :], w0.at[k], loc.at[3 + k]).start()
            pltpu.make_async_copy(
                stream_ref.at[:, :, pl.ds(k * CH, CH)], strm.at[k], loc.at[7 + k]
            ).start()

    @pl.when(phase > 0)
    def _():
        pltpu.make_async_copy(
            proj_ref.at[0, pl.ds(pl.multiple_of(y * CH, CH), CH), :], wbuf.at[phase - 1], loc.at[2]
        ).start()

    pl.semaphore_wait(barrier, count)

    idsrc[...] = jnp.broadcast_to(ids_ref[pl.ds(c, 1), :], (8, T))

    @pl.when(seg < nseg - 1)
    def _():
        remote(idsrc, idh, idsem.at[0], idsem.at[1], phase, seg + 1).start()

    @pl.when(seg == 0)
    def _():
        idh[...] = jnp.full((8, T), -1, jnp.int32)

    def send_params():
        for d in range(1, NY * NC):
            p = (phase + d) % (NY * NC)
            remote(pp_ref.at[p // NC], ppb.at[phase], pps.at[p], wr.at[phase, 2], p, seg).start()

    def send_weights():
        for dy in (2, 1, 3):
            yd = (y + dy) % NY
            remote(
                proj_ref.at[0, pl.ds(pl.multiple_of(yd * CH, CH), CH), :],
                wbuf.at[phase - 1],
                wss.at[yd],
                wr.at[phase, 0],
                yd * NC + c,
                seg,
            ).start()
        remote(
            proj_ref.at[0, pl.ds(pl.multiple_of(y * CH, CH), CH), :],
            wbuf.at[phase - 1],
            wss.at[y],
            wr.at[phase, 1],
            y * NC + 1 - c,
            seg,
        ).start()

    lane = lax.broadcasted_iota(jnp.int32, (T, 128), 1)
    low = lane < 64

    def split_rows(a):
        tiles = []
        for g in range(GROUPS):
            tb = a[:, 128 * (g // 2) : 128 * (g // 2) + 128]
            tc = a[:, 256 + 128 * (g // 2) : 256 + 128 * (g // 2) + 128]
            if g % 2 == 0:
                tiles.append(jnp.where(low, tb, pltpu.roll(tc, 64, 1)))
            else:
                tiles.append(jnp.where(low, pltpu.roll(tb, 64, 1), tc))
        return tiles

    @pl.when(phase == 0)
    def _():
        send_params()
        for k in range(4):
            pltpu.make_async_copy(proj_ref.at[0, pl.ds(k * CH, CH), :], w0.at[k], loc.at[3 + k]).wait()
            pltpu.make_async_copy(
                stream_ref.at[:, :, pl.ds(k * CH, CH)], strm.at[k], loc.at[7 + k]
            ).wait()
        for m in range(MICRO):
            at = LAYERS * m
            acc_bc = jnp.zeros((T, 512), F32)
            acc_s = jnp.zeros((T, 64), F32)
            for k in range(4):
                a = strm[k, m]
                acc_bc = acc_bc + jnp.dot(a, w0[k, :, 0:512], preferred_element_type=F32)
                acc_s = acc_s + jnp.dot(a, w0[k, :, 512:576], preferred_element_type=F32)
            tiles = split_rows(acc_bc)
            st = jnp.transpose(acc_s)
            for g in range(GROUPS):
                bcuo[at, g] = tiles[g].astype(BF16)
                suo[at, g] = st[16 * g : 16 * g + 16]
            for g in range(GROUPS):
                p = g * NC + m
                if p > 0:
                    remote(bcuo.at[at, g], bcu.at[0, 0], p0s.at[p, 0], yr.at[0, 0], p, seg).start()
                    remote(suo.at[at, g], su.at[0, 0], p0s.at[p, 1], yr.at[0, 1], p, seg).start()
        bcu[0, 0] = bcuo[0, 0]
        su[0, 0] = suo[0, 0]

    @pl.when(phase == 1)
    def _():
        send_params()
        send_weights()

    cp_u.wait()
    cp_pp.wait()

    @pl.when(phase > 0)
    def _():
        pltpu.make_async_copy(
            proj_ref.at[0, pl.ds(pl.multiple_of(y * CH, CH), CH), :], wbuf.at[phase - 1], loc.at[2]
        ).wait()

    bcm[0] = jnp.zeros((NY, T, 128), BF16)
    sm[0] = jnp.zeros((NY, 24, 128), F32)
    for s in range(1, NY):
        bcu[0, s] = jnp.zeros((T, 128), BF16)
        su[0, s] = jnp.zeros((16, 128), F32)
    gm[...] = jnp.zeros((T, CH), F32)

    @pl.when(seg > 0)
    def _():
        wait_bytes(idh, idsem.at[1])

    own_row = idsrc[...].astype(F32)
    prior_row = idh[...].astype(F32)
    lane8 = lax.broadcasted_iota(jnp.int32, (8, T), 1)
    row_rep = jnp.broadcast_to(own_row[0:1], (T, T))
    col_rep = jnp.transpose(row_rep)
    t_at = lax.broadcasted_iota(jnp.int32, (T, T), 0)
    msk[0] = jnp.where((row_rep == col_rep) & (t_at >= lane), 1.0, 0.0)
    for k in range(1, KERNEL):
        behind = jnp.where(lane8 < k, pltpu.roll(prior_row, k, 1), pltpu.roll(own_row, k, 1))
        same = jnp.where(behind == own_row, 1.0, 0.0)
        msk[k] = jnp.transpose(jnp.broadcast_to(same[0:1], (T, T)))
    prior_last = jnp.broadcast_to(prior_row[:, T - 1 : T], (8, T))
    own_last = jnp.broadcast_to(own_row[:, T - 1 : T], (8, T))
    sg[1, 0:8] = jnp.where(own_row == prior_last, 1.0, 0.0)
    sg[1, 8:16] = jnp.where(own_row == own_last, 1.0, 0.0)
    sum_up = jnp.where(t_at <= lane, 1.0, 0.0)

    def total_square(lx):
        s = sm[lx, 0, 16:24] + sm[lx, 1, 16:24] + sm[lx, 2, 16:24] + sm[lx, 3, 16:24]
        return lax.rsqrt(s * (1.0 / (CH * GROUPS)) + 1e-05)

    def new_tokens(lx, inv_rep):
        for j in range(NCH):
            cj = pl.ds(128 * j, 128)
            u = ubuf[lx, :, cj].astype(F32) + gm[:, cj] * inv_rep
            ub = u.astype(BF16)
            ubuf[lx + 1, :, cj] = ub
            fbuf[pl.ds(16, T), cj] = ub.astype(F32)

    def send_out(lx):
        there = out_ref.at[0, c, :, pl.ds(pl.multiple_of(y * CH, CH), CH)]

        @pl.when(phase == lx - 1)
        def _():
            pltpu.make_async_copy(ubuf.at[lx + 1], there, outs.at[lx]).start()

        @pl.when(phase != lx - 1)
        def _():
            remote(ubuf.at[lx + 1], there, outs.at[lx], outr.at[phase], lx - 1, seg).start()

    def wait_square(lx):
        wait_bytes(sm.at[lx, pl.ds(0, 3)], yr.at[lx, 3])

    def push_rows(lx, kind, outbuf, inbuf, soutbuf, sinbuf):
        for dy in (2, 1, 3):
            yd = (y + dy) % NY
            remote(
                outbuf.at[lx, yd], inbuf.at[lx, y], ys.at[lx, kind], yr.at[lx, kind], yd * NC + c, seg
            ).start()
        for dy in (2, 1, 3):
            yd = (y + dy) % NY
            remote(
                soutbuf.at[lx, yd],
                sinbuf.at[lx, y],
                ys.at[lx, kind + 1],
                yr.at[lx, kind + 1],
                yd * NC + c,
                seg,
            ).start()

    def conv_rows(l, r0, n):
        for j in range(NCH):
            cj = pl.ds(128 * j, 128)
            acc = fbuf[pl.ds(16 + r0, n), cj] * ppb[l, pl.ds(24 + j, 1), :] + ppb[l, pl.ds(32 + j, 1), :]
            for k in range(1, KERNEL):
                tap = ppb[l, pl.ds(8 * (3 - k) + j, 1), :]
                acc = acc + (fbuf[pl.ds(16 + r0 - k, n), cj] * msk[k, pl.ds(r0, n), :]) * tap
            inp[pl.ds(r0, n), cj] = (acc * (1.0 / (1.0 + jnp.exp(-acc)))).astype(BF16)

    def layer(l, carry):
        @pl.when(phase == l + 2)
        def _():
            send_params()
            send_weights()

        @pl.when((l == 0) & (phase > 0))
        def _():
            wait_bytes(bcu.at[0, 0], yr.at[0, 0])
            wait_bytes(su.at[0, 0], yr.at[0, 1])

        @pl.when(l > 0)
        def _():
            wait_bytes(bcu.at[l, pl.ds(0, 3)], yr.at[l, 0])
            wait_bytes(su.at[l, pl.ds(0, 3)], yr.at[l, 1])
            wait_bytes(bcm.at[l, pl.ds(0, 3)], yr.at[l, 2])
            wait_square(l)

        inv8 = total_square(l)
        inv_rep = jnp.transpose(jnp.broadcast_to(inv8[0:1], (T, T)))
        new_tokens(l, inv_rep)

        @pl.when(seg < nseg - 1)
        def _():
            remote(
                ubuf.at[l + 1, pl.ds(T - 16, 16), :], halo.at[l], hs.at[l], hr.at[l], phase, seg + 1
            ).start()

        @pl.when(l > 0)
        def _():
            send_out(l)

        @pl.when(phase != l)
        def _():
            wait_bytes(ppb.at[l], wr.at[l, 2])

        bc_u = (
            bcu[l, 0].astype(F32) + bcu[l, 1].astype(F32) + bcu[l, 2].astype(F32) + bcu[l, 3].astype(F32)
        )
        bc_m = (
            bcm[l, 0].astype(F32) + bcm[l, 1].astype(F32) + bcm[l, 2].astype(F32) + bcm[l, 3].astype(F32)
        )
        bc = (bc_u + inv_rep * bc_m).astype(BF16)
        bcf = bc.astype(F32)
        s_u = su[l, 0] + su[l, 1] + su[l, 2] + su[l, 3]
        s_m = sm[l, 0, 0:16] + sm[l, 1, 0:16] + sm[l, 2, 0:16] + sm[l, 3, 0:16]
        pre = s_u + inv8[0:1] * s_m + ppb[l, 72:88]
        step = jnp.maximum(pre, 0.0) + jnp.log1p(jnp.exp(-jnp.abs(pre)))
        log_decay = -jnp.exp(ppb[l, 56:72]) * step
        run = jnp.dot(log_decay, sum_up, preferred_element_type=F32, precision=lax.Precision.HIGHEST)
        goes_on = sg[1, 0:1]
        is_last = sg[1, 8:9]
        cgain = jnp.exp(run) * goes_on
        tail = jnp.exp(jnp.broadcast_to(run[:, T - 1 : T], (PER, T)) - run) * is_last * step
        sg[0] = jnp.broadcast_to(cgain[:, T - 1 : T], (PER, T))
        gain8 = jnp.where(
            lane8 < 64, sg[0, pl.ds(0, 8, stride=2), :], sg[0, pl.ds(1, 8, stride=2), :]
        )
        gout[l] = gain8
        grecv[l, x] = gain8
        for d in range(1, NX):
            xd = (x + d) % NX
            remote(gout.at[l], grecv.at[l, x], xs.at[l, 1], xr.at[l, 1], phase, z * NX + xd).start()

        bct = jnp.transpose(bcf)
        bt = bct[0:64]
        cfull = jnp.where(low, pltpu.roll(bcf, 64, 1), 0.0).astype(BF16)
        scores = lax.dot_general(cfull, bc, (((1,), (1,)), ((), ())), preferred_element_type=F32)
        scores = scores * msk[0]
        cols = jnp.transpose(jnp.concatenate([run, cgain, jnp.zeros((T - 2 * PER, T), F32)], axis=0))
        for j in range(NCH):
            for i in range(2):
                h = 2 * j + i
                gap = jnp.broadcast_to(cols[:, h : h + 1], (T, T)) - run[h : h + 1]
                w = scores * (jnp.exp(jnp.minimum(gap, 0.0)) * step[h : h + 1])
                wts[j, :, pl.ds(128 * i, 128)] = w.astype(BF16)
            g0 = jnp.broadcast_to(cols[:, PER + 2 * j : PER + 2 * j + 1], (T, T))
            g1 = jnp.broadcast_to(cols[:, PER + 2 * j + 1 : PER + 2 * j + 2], (T, T))
            gx[:, pl.ds(128 * j, 128)] = jnp.where(low, g0, g1)

        conv_rows(l, 16, T - 16)

        @pl.when(seg > 0)
        def _():
            wait_bytes(halo.at[l], hr.at[l])

        @pl.when(seg == 0)
        def _():
            halo[l] = jnp.zeros((16, CH), BF16)

        fbuf[pl.ds(0, 16), :] = halo[l].astype(F32)
        conv_rows(l, 0, 16)

        low64 = low[0:64]
        for j in range(NCH):
            cj = pl.ds(128 * j, 128)
            left = jnp.concatenate([bt * tail[2 * j : 2 * j + 1], bt * tail[2 * j + 1 : 2 * j + 2]], axis=0)
            both = jnp.dot(left.astype(BF16), inp[:, cj], preferred_element_type=F32)
            st = jnp.where(low64, both[0:64], both[64:128]).astype(BF16)
            for q in range(NX):
                lout[l, q, :, cj] = st[16 * q : 16 * q + 16]
        for d in (2, 1, 3):
            xd = (x + d) % NX
            remote(
                lout.at[l, xd], lrecv.at[l, x], xs.at[l, 0], xr.at[l, 0], phase, z * NX + xd
            ).start()
        lrecv[l, x] = lout[l, x]

        for j in range(NCH):
            cj = pl.ds(128 * j, 128)
            v = inp[:, cj]
            vf = v.astype(F32)
            right = jnp.concatenate([jnp.where(low, vf, 0.0), jnp.where(low, 0.0, vf)], axis=0).astype(BF16)
            intra = jnp.dot(wts[j], right, preferred_element_type=F32)
            m0[:, cj] = intra + ppb[l, pl.ds(48 + j, 1), :] * vf

        wait_bytes(grecv.at[l, pl.ds(0, 3)], xr.at[l, 1])
        wait_bytes(lrecv.at[l, pl.ds(0, 3)], xr.at[l, 0])
        p1 = grecv[l, 0]
        p2 = p1 * grecv[l, 1]
        p3 = p2 * grecv[l, 2]
        ggout[l] = p3 * grecv[l, 3]
        ga = grecv[l, 1]
        gb = grecv[l, 2]
        gc = grecv[l, 3]
        for j in range(NCH):
            cj = pl.ds(128 * j, 128)
            r1 = lrecv[l, 0, :, cj].astype(F32)
            r2 = lrecv[l, 1, :, cj].astype(F32) + ga[j : j + 1] * r1
            r3 = lrecv[l, 2, :, cj].astype(F32) + gb[j : j + 1] * r2
            rt = lrecv[l, 3, :, cj].astype(F32) + gc[j : j + 1] * r3
            rb[0, :, cj] = r1
            rb[1, :, cj] = r2
            rb[2, :, cj] = r3
            tout[l, :, cj] = rt.astype(BF16)
        for d in range(REACH, 0, -1):

            @pl.when(z + d < nz)
            def _(d=d):
                to = (z + d) * NX + x
                remote(
                    ggout.at[l], ggrecv.at[l, d - 1], zs.at[l, REACH + d - 1], zr.at[l, REACH + d - 1], phase, to
                ).start()
                remote(tout.at[l], trecv.at[l, d - 1], zs.at[l, d - 1], zr.at[l, d - 1], phase, to).start()

        n = l + 1
        yo = n // NC
        co = n % NC

        @pl.when(n < LAYERS)
        def _():
            @pl.when((c == co) & (y != yo))
            def _():
                wait_bytes(wbuf.at[l], wr.at[n, 0])
                remote(wbuf.at[l], wbuf.at[l], wrs.at[l], wr.at[n, 1], y * NC + 1 - c, seg).start()

            @pl.when(c != co)
            def _():
                wait_bytes(wbuf.at[l], wr.at[n, 1])

            a = ubuf[l + 1]
            tiles = split_rows(jnp.dot(a, wbuf[l, :, 0:512], preferred_element_type=F32))
            st = jnp.transpose(jnp.dot(a, wbuf[l, :, 512:576], preferred_element_type=F32))
            for g in range(GROUPS):
                bcuo[n, g] = tiles[g].astype(BF16)
                suo[n, g] = st[16 * g : 16 * g + 16]
            bcu[n, y] = bcuo[n, y]
            su[n, y] = suo[n, y]
            push_rows(n, 0, bcuo, bcu, suo, su)

        for d in range(1, REACH + 1):

            @pl.when(z >= d)
            def _(d=d):
                wait_bytes(ggrecv.at[l, d - 1], zr.at[l, REACH + d - 1])
                wait_bytes(trecv.at[l, d - 1], zr.at[l, d - 1])

            @pl.when(z < d)
            def _(d=d):
                ggrecv[l, d - 1] = jnp.zeros((8, 128), F32)
                trecv[l, d - 1] = jnp.zeros((16, CH), BF16)

        for j in range(NCH):
            cj = pl.ds(128 * j, 128)
            e = trecv[l, 3, :, cj].astype(F32)
            for d in (2, 1, 0):
                e = trecv[l, d, :, cj].astype(F32) + ggrecv[l, d, pl.ds(j, 1), :] * e
            eout[l, 0, :, cj] = e.astype(BF16)
            eout[l, 1, :, cj] = (rb[0, :, cj] + p1[j : j + 1] * e).astype(BF16)
            eout[l, 2, :, cj] = (rb[1, :, cj] + p2[j : j + 1] * e).astype(BF16)
            eout[l, 3, :, cj] = (rb[2, :, cj] + p3[j : j + 1] * e).astype(BF16)
        for d in (2, 1, 3):
            xd = (x + d) % NX
            remote(
                eout.at[l, xd], ent.at[l, x], xs.at[l, 2], xr.at[l, 2], phase, z * NX + xd
            ).start()
        ent[l, x] = eout[l, x]

        wait_bytes(ent.at[l, pl.ds(0, 3)], xr.at[l, 2])
        cs = cfull[:, 0:64]
        sq = jnp.zeros((T, 128), F32)
        for j in range(NCH):
            cj = pl.ds(128 * j, 128)
            part = jnp.dot(cs, ent[l, :, :, cj].reshape(STATE, 128), preferred_element_type=F32)
            mixed = m0[:, cj] + part * gx[:, cj]
            sq = sq + mixed * mixed
            scaled = ppb[l, pl.ds(40 + j, 1), :] * mixed
            gm[:, cj] = scaled
            gmb[:, cj] = scaled.astype(BF16)
        sq_row = jnp.broadcast_to(jnp.sum(jnp.transpose(sq), axis=0, keepdims=True), (8, T))
        for g in range(GROUPS):
            smo[n, g, 16:24] = sq_row

        @pl.when(n < LAYERS)
        def _():
            a = gmb[...]
            tiles = split_rows(jnp.dot(a, wbuf[l, :, 0:512], preferred_element_type=F32))
            st = jnp.transpose(jnp.dot(a, wbuf[l, :, 512:576], preferred_element_type=F32))
            for g in range(GROUPS):
                bcmo[n, g] = tiles[g].astype(BF16)
                smo[n, g, 0:16] = st[16 * g : 16 * g + 16]
            bcm[n, y] = bcmo[n, y]
            sm[n, y] = smo[n, y]
            push_rows(n, 2, bcmo, bcm, smo, sm)

        @pl.when(n == LAYERS)
        def _():
            for g in range(GROUPS):
                smo[n, g, 0:16] = jnp.zeros((16, 128), F32)
            sm[n, y] = smo[n, y]
            for dy in (2, 1, 3):
                yd = (y + dy) % NY
                remote(
                    smo.at[n, yd], sm.at[n, y], ys.at[n, 3], yr.at[n, 3], yd * NC + c, seg
                ).start()

        return carry

    lax.fori_loop(0, LAYERS, layer, 0)

    wait_square(LAYERS)
    inv8 = total_square(LAYERS)
    new_tokens(LAYERS, jnp.transpose(jnp.broadcast_to(inv8[0:1], (T, T))))
    send_out(LAYERS)

    def drain(l, carry):
        n = l + 1

        @pl.when(n < LAYERS)
        def _():
            wait_bytes(bcuo.at[n, pl.ds(0, 3)], ys.at[n, 0])
            wait_bytes(suo.at[n, pl.ds(0, 3)], ys.at[n, 1])
            wait_bytes(bcmo.at[n, pl.ds(0, 3)], ys.at[n, 2])

        wait_bytes(smo.at[n, pl.ds(0, 3)], ys.at[n, 3])
        wait_bytes(ubuf.at[n + 1], outs.at[n])
        wait_bytes(lout.at[l, pl.ds(0, 3)], xs.at[l, 0])
        wait_bytes(grecv.at[l, pl.ds(0, 3)], xs.at[l, 1])
        wait_bytes(eout.at[l, pl.ds(0, 3)], xs.at[l, 2])
        for d in range(1, REACH + 1):

            @pl.when(z + d < nz)
            def _(d=d):
                wait_bytes(ggout.at[l], zs.at[l, REACH + d - 1])
                wait_bytes(tout.at[l], zs.at[l, d - 1])

        @pl.when(seg < nseg - 1)
        def _():
            wait_bytes(halo.at[l], hs.at[l])

        @pl.when((n < LAYERS) & (c == n % NC) & (y != n // NC))
        def _():
            wait_bytes(wbuf.at[l], wrs.at[l])

        @pl.when(phase != l)
        def _():
            wait_bytes(ubuf.at[0], outr.at[l])
            wait_bytes(ppb.at[l], pps.at[l])

        return carry

    lax.fori_loop(0, LAYERS, drain, 0)

    @pl.when(phase > 0)
    def _():
        for yd in range(NY):
            wait_bytes(wbuf.at[0], wss.at[yd])

    @pl.when(phase == 0)
    def _():
        for p in range(1, NY * NC):
            wait_bytes(bcuo.at[0, 0], p0s.at[p, 0])
            wait_bytes(suo.at[0, 0], p0s.at[p, 1])

    @pl.when(seg < nseg - 1)
    def _():
        wait_bytes(idsrc, idsem.at[0])


def body(
    stream, doc_ids, in_proj, conv_weight, conv_bias, decay_log, step_bias, skip_gain, norm_gain
):
    nseg = lax.axis_size("seg")
    nz = nseg // NX

    def rows(a):
        return a.reshape(-1, GROUPS, NCH, 128).transpose(1, 0, 2, 3).reshape(GROUPS, -1, 128)

    def wide(a):
        return jnp.broadcast_to(a.reshape(GROUPS, PER, 1), (GROUPS, PER, 128))

    params = jnp.concatenate(
        [
            rows(conv_weight[0]),
            rows(conv_bias),
            rows(norm_gain),
            rows(jnp.repeat(skip_gain, HEAD_DIM, axis=1)),
            wide(decay_log),
            wide(step_bias),
        ],
        axis=1,
    )
    vmem = pltpu.VMEM
    dma = pltpu.SemaphoreType.DMA
    n1 = LAYERS + 1
    return pl.pallas_call(
        functools.partial(kernel, nz),
        out_shape=jax.ShapeDtypeStruct((1, MICRO, T, CH * GROUPS), BF16),
        in_specs=[
            pl.BlockSpec(memory_space=pl.ANY),
            pl.BlockSpec(memory_space=pltpu.VMEM),
            pl.BlockSpec(memory_space=pl.ANY),
            pl.BlockSpec(memory_space=pl.ANY),
        ],
        out_specs=pl.BlockSpec(memory_space=pl.ANY),
        scratch_shapes=[
            vmem((LAYERS - 1, CH, PROJ), BF16),
            vmem((4, CH, PROJ), BF16),
            vmem((4, MICRO, T, CH), BF16),
            vmem((LAYERS + 2, T, CH), BF16),
            vmem((T, CH), F32),
            vmem((T, CH), BF16),
            vmem((LAYERS, 88, 128), F32),
            vmem((8, T), jnp.int32),
            vmem((8, T), jnp.int32),
            vmem((KERNEL, T, T), F32),
            vmem((LAYERS, 16, CH), BF16),
            vmem((T + 16, CH), F32),
            vmem((T, CH), BF16),
            vmem((NCH, T, 256), BF16),
            vmem((n1, NY, T, 128), BF16),
            vmem((n1, NY, T, 128), BF16),
            vmem((n1, NY, T, 128), BF16),
            vmem((n1, NY, T, 128), BF16),
            vmem((n1, NY, 16, 128), F32),
            vmem((n1, NY, 24, 128), F32),
            vmem((n1, NY, 16, 128), F32),
            vmem((n1, NY, 24, 128), F32),
            vmem((2, 16, 128), F32),
            vmem((LAYERS, NX, 16, CH), BF16),
            vmem((LAYERS, NX, 16, CH), BF16),
            vmem((LAYERS, 8, 128), F32),
            vmem((LAYERS, NX, 8, 128), F32),
            vmem((LAYERS, 16, CH), BF16),
            vmem((LAYERS, 8, 128), F32),
            vmem((LAYERS, REACH, 16, CH), BF16),
            vmem((LAYERS, REACH, 8, 128), F32),
            vmem((3, 16, CH), F32),
            vmem((LAYERS, NX, 16, CH), BF16),
            vmem((LAYERS, NX, 16, CH), BF16),
            vmem((T, CH), F32),
            vmem((T, CH), F32),
            dma((n1, 4)),
            dma((n1, 4)),
            dma((NY * NC, 2)),
            dma((LAYERS, 3)),
            dma((LAYERS, 3)),
            dma((LAYERS, 2 * REACH)),
            dma((LAYERS, 2 * REACH)),
            dma((LAYERS,)),
            dma((LAYERS,)),
            dma((LAYERS, 3)),
            dma((NY,)),
            dma((LAYERS,)),
            dma((NY * NC,)),
            dma((NY * NC,)),
            dma((n1,)),
            dma((2,)),
            dma((11,)),
        ],
        compiler_params=pltpu.CompilerParams(
            collective_id=0, has_side_effects=True, vmem_limit_bytes=60 * 1024 * 1024
        ),
    )(stream, doc_ids, in_proj, params)


def solution(mesh):
    placed = (
        P(None, "seg", None),
        P(None, "seg"),
        P("phase", None, None),
        P("phase", None, None),
        P("phase", None),
        P("phase", None),
        P("phase", None),
        P("phase", None),
        P("phase", None),
    )
    return jax.shard_map(
        body, mesh=mesh, in_specs=placed, out_specs=P("phase", None, "seg", None), check_vma=False
    )
```

time: 1570 us -> 311 us (0.20)
  the two profiles are of different devices: /device:TPU:1 before, /device:TPU:249 now
where the time goes in v1:
time: 311 us; the launch traced here: 310 us
  Pallas kernels  292 us (94%)
  local copies, waits for them, and re-layouts  14.2 us (5%)
  other arithmetic  3.95 us (1%)
    pallas_call x1, Pallas kernels, body(): pl.pallas_call(functools.partial(kernel, nz), out_shape=jax.ShapeDtypeStr...  292 us
    unnamed x10, local copies, waits for them, and re-layouts  13.7 us

profile of v1, /device:TPU:249, one launch (start us, length us, event | category | flops | bytes accessed | tf_op | source)
XLA Modules:
  0.0 310.2 jit_solution(5259971094542540719)
XLA Ops:
  0.0 0.5 broadcast.12
  0.5 1.3 reduce.10
  1.8 1.3 reduce.11
  3.1 1.3 reduce.9
  4.5 0.1 broadcast_in_dim.26
  4.5 0.1 broadcast_in_dim.24
  4.6 0.1 broadcast_in_dim.21
  4.7 0.1 broadcast_in_dim.22
  4.8 0.1 broadcast_in_dim.23
  4.9 0.8 bitcast_dynamic-update-slice_fusion
  5.8 0.7 constant_dynamic-update-slice_fusion.2
  6.5 0.7 constant_dynamic-update-slice_fusion.1
  7.2 0.1 broadcast_dynamic-update-slice_fusion.1
  7.3 0.1 broadcast_dynamic-update-slice_fusion.pp_ref
  7.4 0.0 copy-start
  7.4 7.7 %copy.13.proj_ref = bf16[1,4096,576]{2,1,0:T(8,128)(2,1)} copy(bf16[1,4096,576]{1,2,0:T(8,128)(2,1)} %param.11) | data formatting | bytes 9437184 | tf_op args[2]
  15.1 0.0 copy-done
  15.1 292.0 %shard_map.91 = bf16[1,2,128,4096]{3,2,1,0:T(8,128)(2,1)} custom-call(bf16[2,128,4096]{2,1,0:T(8,128)(2,1)} %stream_ref.1, s32[2,128]{1,0:T(2,128)} %ids_ref.1, bf16[1,4096,576]{2,1,0:T(8,128)(2,1)} %copy.13.proj_ref, f32[4,88,128]{2,1,0:T(8,128)} %copy-done), custom_call_target="tpu_custom_call" | custom-call | tf_op jit(solution)/shard_map/pallas_call | solution.py:653
  307.0 3.1 %copy.24 = bf16[1,2,128,4096]{3,2,1,0:T(8,128)(2,1)} copy(bf16[1,2,128,4096]{3,2,1,0:T(8,128)(2,1)} %shard_map.91) | data formatting | bytes 4194304
  (1 shorter events, 0.0 us)
Async XLA Ops:
  7.4 7.7 %copy-start = (f32[4,88,128]{2,1,0:T(8,128)}, f32[4,88,128]{2,1,0:T(8,128)S(1)}, u32[]{:S(2)}) copy-start(f32[4,88,128]{2,1,0:T(8,128)S(1)} %broadcast_dynamic-update-slice_fusion.pp_ref) | copy-start | bytes 540676

commit v2 on v1

--- a/solution.py
+++ b/solution.py
@@ -23,6 +23,8 @@
 NCH = 8
 REACH = 4
 PROJ = 576
+WPART = 144
+WHALF = 80
 MESH = pl.DeviceIdType.MESH
 F32 = jnp.float32
 BF16 = jnp.bfloat16
@@ -37,7 +39,12 @@
     stream_ref,
     ids_ref,
     proj_ref,
-    pp_ref,
+    convw_ref,
+    convb_ref,
+    decay_ref,
+    stepb_ref,
+    skip_ref,
+    norm_ref,
     out_ref,
     wbuf,
     w0,
@@ -45,6 +52,9 @@
     ubuf,
     gm,
     gmb,
+    pps,
+    pph,
+    p0,
     ppb,
     idsrc,
     idh,
@@ -87,7 +97,8 @@
     wr,
     wss,
     wrs,
-    pps,
+    wxs,
+    ppsem,
     outr,
     outs,
     idsem,
@@ -134,22 +145,43 @@
         stream_ref.at[c, :, pl.ds(pl.multiple_of(y * CH, CH), CH)], ubuf.at[0], loc.at[0]
     )
     cp_u.start()
-    cp_pp = pltpu.make_async_copy(pp_ref.at[y], ppb.at[phase], loc.at[1])
-    cp_pp.start()
+    def quarter(g):
+        return proj_ref.at[0, :, pl.ds(pl.multiple_of(g * CH, CH), CH)]
+
+    cp_w0 = pltpu.make_async_copy(proj_ref.at[0], w0, loc.at[1])
+    cp_s0 = pltpu.make_async_copy(stream_ref, strm, loc.at[3])
 
     @pl.when(phase == 0)
     def _():
-        for k in range(4):
-            pltpu.make_async_copy(proj_ref.at[0, pl.ds(k * CH, CH), :], w0.at[k], loc.at[3 + k]).start()
-            pltpu.make_async_copy(
-                stream_ref.at[:, :, pl.ds(k * CH, CH)], strm.at[k], loc.at[7 + k]
-            ).start()
+        cp_w0.start()
+        cp_s0.start()
 
     @pl.when(phase > 0)
     def _():
-        pltpu.make_async_copy(
-            proj_ref.at[0, pl.ds(pl.multiple_of(y * CH, CH), CH), :], wbuf.at[phase - 1], loc.at[2]
-        ).start()
+        pltpu.make_async_copy(quarter(y), wbuf.at[phase - 1], loc.at[2]).start()
+
+    low8 = lax.broadcasted_iota(jnp.int32, (8, 128), 1) < 64
+    for g in range(GROUPS):
+        for j in range(NCH):
+            cj = pl.ds(CH * g + 128 * j, 128)
+            for k in range(KERNEL):
+                pps[g, pl.ds(8 * k + j, 1), :] = convw_ref[0, pl.ds(k, 1), cj]
+            pps[g, pl.ds(32 + j, 1), :] = convb_ref[:, cj]
+            pps[g, pl.ds(40 + j, 1), :] = norm_ref[:, cj]
+
+    def per_head(ref):
+        return jnp.transpose(jnp.broadcast_to(ref[...], (128, HEADS)))
+
+    pph[...] = per_head(skip_ref)
+    decay_rows = per_head(decay_ref)
+    stepb_rows = per_head(stepb_ref)
+    for g in range(GROUPS):
+        pps[g, 48:56] = jnp.where(
+            low8, pph[pl.ds(PER * g, 8, stride=2), :], pph[pl.ds(PER * g + 1, 8, stride=2), :]
+        )
+        pps[g, 56:72] = decay_rows[PER * g : PER * g + PER]
+        pps[g, 72:88] = stepb_rows[PER * g : PER * g + PER]
+    ppb[phase] = pps[y]
 
     pl.semaphore_wait(barrier, count)
 
@@ -166,64 +198,89 @@
     def send_params():
         for d in range(1, NY * NC):
             p = (phase + d) % (NY * NC)
-            remote(pp_ref.at[p // NC], ppb.at[phase], pps.at[p], wr.at[phase, 2], p, seg).start()
+            remote(pps.at[p // NC], ppb.at[phase], ppsem.at[p], wr.at[phase, 6], p, seg).start()
+
+    def part(n, i, r0, rows):
+        return wbuf.at[n - 1, pl.ds(pl.multiple_of(i * WPART + r0, 16), rows), :]
 
     def send_weights():
+        rows = pl.ds(pl.multiple_of(x * WPART, 16), WPART)
         for dy in (2, 1, 3):
             yd = (y + dy) % NY
             remote(
-                proj_ref.at[0, pl.ds(pl.multiple_of(yd * CH, CH), CH), :],
-                wbuf.at[phase - 1],
+                proj_ref.at[0, rows, pl.ds(pl.multiple_of(yd * CH, CH), CH)],
+                part(phase, x, 0, WPART),
                 wss.at[yd],
                 wr.at[phase, 0],
                 yd * NC + c,
                 seg,
             ).start()
-        remote(
-            proj_ref.at[0, pl.ds(pl.multiple_of(y * CH, CH), CH), :],
-            wbuf.at[phase - 1],
-            wss.at[y],
-            wr.at[phase, 1],
-            y * NC + 1 - c,
-            seg,
-        ).start()
+        remote(quarter(y), wbuf.at[phase - 1], wss.at[y], wr.at[phase, 5], y * NC + 1 - c, seg).start()
+
+    def relays(n):
+        return (n < LAYERS) & (c == n % NC) & (y != n // NC)
+
+    right = z * NX + (x + 1) % NX
+    left = z * NX + (x + NX - 1) % NX
+
+    def weights_1(n):
+        @pl.when(relays(n))
+        def _():
+            mine = part(n, x, 0, WPART)
+            wait_bytes(mine, wr.at[n, 0])
+            remote(mine, mine, wxs.at[n, 0], wr.at[n, 1], phase, right).start()
+            remote(mine, mine, wxs.at[n, 1], wr.at[n, 2], phase, left).start()
+
+    def weights_2(n):
+        @pl.when(relays(n))
+        def _():
+            wait_bytes(part(n, x, 0, WPART), wr.at[n, 1])
+            first = part(n, (x + NX - 1) % NX, 0, WHALF)
+            remote(first, first, wxs.at[n, 2], wr.at[n, 3], phase, right).start()
+            wait_bytes(part(n, x, 0, WPART), wr.at[n, 2])
+            last = part(n, (x + 1) % NX, WHALF, WPART - WHALF)
+            remote(last, last, wxs.at[n, 3], wr.at[n, 4], phase, left).start()
+
+    def weights_3(n):
+        @pl.when(relays(n))
+        def _():
+            wait_bytes(part(n, x, 0, WHALF), wr.at[n, 3])
+            wait_bytes(part(n, x, 0, WPART - WHALF), wr.at[n, 4])
+            whole = wbuf.at[n - 1]
+            remote(whole, whole, wrs.at[n], wr.at[n, 5], y * NC + 1 - c, seg).start()
+
+        @pl.when((n < LAYERS) & (c != n % NC))
+        def _():
+            wait_bytes(wbuf.at[n - 1], wr.at[n, 5])
 
     lane = lax.broadcasted_iota(jnp.int32, (T, 128), 1)
     low = lane < 64
 
-    def split_rows(a):
-        tiles = []
-        for g in range(GROUPS):
-            tb = a[:, 128 * (g // 2) : 128 * (g // 2) + 128]
-            tc = a[:, 256 + 128 * (g // 2) : 256 + 128 * (g // 2) + 128]
-            if g % 2 == 0:
-                tiles.append(jnp.where(low, tb, pltpu.roll(tc, 64, 1)))
-            else:
-                tiles.append(jnp.where(low, pltpu.roll(tb, 64, 1), tc))
-        return tiles
+    def product(w, a):
+        return lax.dot_general(w, a, (((1,), (1,)), ((), ())), preferred_element_type=F32)
+
+    def rows_of(a, g):
+        return jnp.concatenate(
+            [a[64 * g : 64 * g + 64], a[256 + 64 * g : 320 + 64 * g]], axis=0
+        ).astype(BF16)
 
     @pl.when(phase == 0)
     def _():
         send_params()
-        for k in range(4):
-            pltpu.make_async_copy(proj_ref.at[0, pl.ds(k * CH, CH), :], w0.at[k], loc.at[3 + k]).wait()
-            pltpu.make_async_copy(
-                stream_ref.at[:, :, pl.ds(k * CH, CH)], strm.at[k], loc.at[7 + k]
-            ).wait()
+        cp_w0.wait()
+        cp_s0.wait()
+        both = strm[...].reshape(MICRO * T, CH * GROUPS)
+        for r in range(4):
+            rr = pl.ds(WPART * r, WPART)
+            p0[rr, :] = product(w0[rr, :], both)
         for m in range(MICRO):
             at = LAYERS * m
-            acc_bc = jnp.zeros((T, 512), F32)
-            acc_s = jnp.zeros((T, 64), F32)
-            for k in range(4):
-                a = strm[k, m]
-                acc_bc = acc_bc + jnp.dot(a, w0[k, :, 0:512], preferred_element_type=F32)
-                acc_s = acc_s + jnp.dot(a, w0[k, :, 512:576], preferred_element_type=F32)
-            tiles = split_rows(acc_bc)
-            st = jnp.transpose(acc_s)
+            cm = pl.ds(T * m, T)
             for g in range(GROUPS):
-                bcuo[at, g] = tiles[g].astype(BF16)
-                suo[at, g] = st[16 * g : 16 * g + 16]
-            for g in range(GROUPS):
+                bcuo[at, g, 0:64] = p0[pl.ds(64 * g, 64), cm].astype(BF16)
+                bcuo[at, g, 64:128] = p0[pl.ds(256 + 64 * g, 64), cm].astype(BF16)
+                suo[at, g] = p0[pl.ds(512 + 16 * g, 16), cm]
+            for g in (2, 1, 3, 0):
                 p = g * NC + m
                 if p > 0:
                     remote(bcuo.at[at, g], bcu.at[0, 0], p0s.at[p, 0], yr.at[0, 0], p, seg).start()
@@ -231,19 +288,16 @@
         bcu[0, 0] = bcuo[0, 0]
         su[0, 0] = suo[0, 0]
 
-    @pl.when(phase == 1)
+    @pl.when((phase == 1) | (phase == 2))
     def _():
         send_params()
         send_weights()
 
     cp_u.wait()
-    cp_pp.wait()
 
     @pl.when(phase > 0)
     def _():
-        pltpu.make_async_copy(
-            proj_ref.at[0, pl.ds(pl.multiple_of(y * CH, CH), CH), :], wbuf.at[phase - 1], loc.at[2]
-        ).wait()
+        pltpu.make_async_copy(quarter(y), wbuf.at[phase - 1], loc.at[2]).wait()
 
     bcm[0] = jnp.zeros((NY, T, 128), BF16)
     sm[0] = jnp.zeros((NY, 24, 128), F32)
@@ -272,6 +326,7 @@
     sg[1, 0:8] = jnp.where(own_row == prior_last, 1.0, 0.0)
     sg[1, 8:16] = jnp.where(own_row == own_last, 1.0, 0.0)
     sum_up = jnp.where(t_at <= lane, 1.0, 0.0)
+    weights_1(1)
 
     def total_square(lx):
         s = sm[lx, 0, 16:24] + sm[lx, 1, 16:24] + sm[lx, 2, 16:24] + sm[lx, 3, 16:24]
@@ -326,7 +381,7 @@
             inp[pl.ds(r0, n), cj] = (acc * (1.0 / (1.0 + jnp.exp(-acc)))).astype(BF16)
 
     def layer(l, carry):
-        @pl.when(phase == l + 2)
+        @pl.when(phase == l + 3)
         def _():
             send_params()
             send_weights()
@@ -359,7 +414,7 @@
 
         @pl.when(phase != l)
         def _():
-            wait_bytes(ppb.at[l], wr.at[l, 2])
+            wait_bytes(ppb.at[l], wr.at[l, 6])
 
         bc_u = (
             bcu[l, 0].astype(F32) + bcu[l, 1].astype(F32) + bcu[l, 2].astype(F32) + bcu[l, 3].astype(F32)
@@ -367,8 +422,9 @@
         bc_m = (
             bcm[l, 0].astype(F32) + bcm[l, 1].astype(F32) + bcm[l, 2].astype(F32) + bcm[l, 3].astype(F32)
         )
-        bc = (bc_u + inv_rep * bc_m).astype(BF16)
-        bcf = bc.astype(F32)
+        bc = (bc_u + inv8[0:1] * bc_m).astype(BF16)
+        bt = bc[0:64].astype(F32)
+        cs = jnp.transpose(bc[64:128].astype(F32)).astype(BF16)
         s_u = su[l, 0] + su[l, 1] + su[l, 2] + su[l, 3]
         s_m = sm[l, 0, 0:16] + sm[l, 1, 0:16] + sm[l, 2, 0:16] + sm[l, 3, 0:16]
         pre = s_u + inv8[0:1] * s_m + ppb[l, 72:88]
@@ -389,10 +445,7 @@
             xd = (x + d) % NX
             remote(gout.at[l], grecv.at[l, x], xs.at[l, 1], xr.at[l, 1], phase, z * NX + xd).start()
 
-        bct = jnp.transpose(bcf)
-        bt = bct[0:64]
-        cfull = jnp.where(low, pltpu.roll(bcf, 64, 1), 0.0).astype(BF16)
-        scores = lax.dot_general(cfull, bc, (((1,), (1,)), ((), ())), preferred_element_type=F32)
+        scores = jnp.dot(cs, bc[0:64], preferred_element_type=F32)
         scores = scores * msk[0]
         cols = jnp.transpose(jnp.concatenate([run, cgain, jnp.zeros((T - 2 * PER, T), F32)], axis=0))
         for j in range(NCH):
@@ -433,6 +486,10 @@
             ).start()
         lrecv[l, x] = lout[l, x]
 
+        @pl.when(l == 0)
+        def _():
+            weights_2(1)
+
         for j in range(NCH):
             cj = pl.ds(128 * j, 128)
             v = inp[:, cj]
@@ -471,26 +528,15 @@
                 remote(tout.at[l], trecv.at[l, d - 1], zs.at[l, d - 1], zr.at[l, d - 1], phase, to).start()
 
         n = l + 1
-        yo = n // NC
-        co = n % NC
 
         @pl.when(n < LAYERS)
         def _():
-            @pl.when((c == co) & (y != yo))
-            def _():
-                wait_bytes(wbuf.at[l], wr.at[n, 0])
-                remote(wbuf.at[l], wbuf.at[l], wrs.at[l], wr.at[n, 1], y * NC + 1 - c, seg).start()
-
-            @pl.when(c != co)
-            def _():
-                wait_bytes(wbuf.at[l], wr.at[n, 1])
-
-            a = ubuf[l + 1]
-            tiles = split_rows(jnp.dot(a, wbuf[l, :, 0:512], preferred_element_type=F32))
-            st = jnp.transpose(jnp.dot(a, wbuf[l, :, 512:576], preferred_element_type=F32))
+            weights_1(n + 1)
+            weights_3(n)
+            a = product(wbuf[l], ubuf[l + 1])
             for g in range(GROUPS):
-                bcuo[n, g] = tiles[g].astype(BF16)
-                suo[n, g] = st[16 * g : 16 * g + 16]
+                bcuo[n, g] = rows_of(a, g)
+                suo[n, g] = a[512 + 16 * g : 528 + 16 * g]
             bcu[n, y] = bcuo[n, y]
             su[n, y] = suo[n, y]
             push_rows(n, 0, bcuo, bcu, suo, su)
@@ -524,7 +570,6 @@
         ent[l, x] = eout[l, x]
 
         wait_bytes(ent.at[l, pl.ds(0, 3)], xr.at[l, 2])
-        cs = cfull[:, 0:64]
         sq = jnp.zeros((T, 128), F32)
         for j in range(NCH):
             cj = pl.ds(128 * j, 128)
@@ -540,12 +585,10 @@
 
         @pl.when(n < LAYERS)
         def _():
-            a = gmb[...]
-            tiles = split_rows(jnp.dot(a, wbuf[l, :, 0:512], preferred_element_type=F32))
-            st = jnp.transpose(jnp.dot(a, wbuf[l, :, 512:576], preferred_element_type=F32))
+            a = product(wbuf[l], gmb[...])
             for g in range(GROUPS):
-                bcmo[n, g] = tiles[g].astype(BF16)
-                smo[n, g, 0:16] = st[16 * g : 16 * g + 16]
+                bcmo[n, g] = rows_of(a, g)
+                smo[n, g, 0:16] = a[512 + 16 * g : 528 + 16 * g]
             bcm[n, y] = bcmo[n, y]
             sm[n, y] = smo[n, y]
             push_rows(n, 2, bcmo, bcm, smo, sm)
@@ -561,6 +604,7 @@
                     smo.at[n, yd], sm.at[n, y], ys.at[n, 3], yr.at[n, 3], yd * NC + c, seg
                 ).start()
 
+        weights_2(n + 1)
         return carry
 
     lax.fori_loop(0, LAYERS, layer, 0)
@@ -595,14 +639,16 @@
         def _():
             wait_bytes(halo.at[l], hs.at[l])
 
-        @pl.when((n < LAYERS) & (c == n % NC) & (y != n // NC))
-        def _():
-            wait_bytes(wbuf.at[l], wrs.at[l])
+        @pl.when(relays(n))
+        def _():
+            wait_bytes(wbuf.at[l], wrs.at[n])
+            for i, rows in enumerate((WPART, WPART, WHALF, WPART - WHALF)):
+                wait_bytes(part(n, x, 0, rows), wxs.at[n, i])
 
         @pl.when(phase != l)
         def _():
             wait_bytes(ubuf.at[0], outr.at[l])
-            wait_bytes(ppb.at[l], pps.at[l])
+            wait_bytes(ppb.at[l], ppsem.at[l])
 
         return carry
 
@@ -610,8 +656,9 @@
 
     @pl.when(phase > 0)
     def _():
-        for yd in range(NY):
-            wait_bytes(wbuf.at[0], wss.at[yd])
+        for dy in range(1, NY):
+            wait_bytes(part(1, x, 0, WPART), wss.at[(y + dy) % NY])
+        wait_bytes(wbuf.at[0], wss.at[y])
 
     @pl.when(phase == 0)
     def _():
@@ -630,23 +677,6 @@
     nseg = lax.axis_size("seg")
     nz = nseg // NX
 
-    def rows(a):
-        return a.reshape(-1, GROUPS, NCH, 128).transpose(1, 0, 2, 3).reshape(GROUPS, -1, 128)
-
-    def wide(a):
-        return jnp.broadcast_to(a.reshape(GROUPS, PER, 1), (GROUPS, PER, 128))
-
-    params = jnp.concatenate(
-        [
-            rows(conv_weight[0]),
-            rows(conv_bias),
-            rows(norm_gain),
-            rows(jnp.repeat(skip_gain, HEAD_DIM, axis=1)),
-            wide(decay_log),
-            wide(step_bias),
-        ],
-        axis=1,
-    )
     vmem = pltpu.VMEM
     dma = pltpu.SemaphoreType.DMA
     n1 = LAYERS + 1
@@ -657,16 +687,19 @@
             pl.BlockSpec(memory_space=pl.ANY),
             pl.BlockSpec(memory_space=pltpu.VMEM),
             pl.BlockSpec(memory_space=pl.ANY),
-            pl.BlockSpec(memory_space=pl.ANY),
-        ],
+        ]
+        + [pl.BlockSpec(memory_space=pltpu.VMEM)] * 6,
         out_specs=pl.BlockSpec(memory_space=pl.ANY),
         scratch_shapes=[
-            vmem((LAYERS - 1, CH, PROJ), BF16),
-            vmem((4, CH, PROJ), BF16),
-            vmem((4, MICRO, T, CH), BF16),
+            vmem((LAYERS - 1, PROJ, CH), BF16),
+            vmem((PROJ, CH * GROUPS), BF16),
+            vmem((MICRO, T, CH * GROUPS), BF16),
             vmem((LAYERS + 2, T, CH), BF16),
             vmem((T, CH), F32),
             vmem((T, CH), BF16),
+            vmem((GROUPS, 88, 128), F32),
+            vmem((HEADS, 128), F32),
+            vmem((PROJ, MICRO * T), F32),
             vmem((LAYERS, 88, 128), F32),
             vmem((8, T), jnp.int32),
             vmem((8, T), jnp.int32),
@@ -706,19 +739,30 @@
             dma((LAYERS, 2 * REACH)),
             dma((LAYERS,)),
             dma((LAYERS,)),
-            dma((LAYERS, 3)),
+            dma((LAYERS, 7)),
             dma((NY,)),
             dma((LAYERS,)),
+            dma((LAYERS, 4)),
             dma((NY * NC,)),
             dma((NY * NC,)),
             dma((n1,)),
             dma((2,)),
-            dma((11,)),
+            dma((4,)),
         ],
         compiler_params=pltpu.CompilerParams(
             collective_id=0, has_side_effects=True, vmem_limit_bytes=60 * 1024 * 1024
         ),
-    )(stream, doc_ids, in_proj, params)
+    )(
+        stream,
+        doc_ids,
+        jnp.swapaxes(in_proj, 1, 2),
+        conv_weight,
+        conv_bias,
+        decay_log,
+        step_bias,
+        skip_gain,
+        norm_gain,
+    )
 
 
 def solution(mesh):

time: 311 us -> 206 us (0.66)
  Pallas kernels: 292 us -> 203 us
  local copies, waits for them, and re-layouts: 14.2 us -> 3.13 us
  other arithmetic: 3.95 us -> 0 us
    pallas_call x1, Pallas kernels: 292 us -> 203 us  [body(): pl.pallas_call(functools.partial(kernel, nz), out_shape=jax.ShapeDtypeStr...]
    unnamed x10 -> x1, local copies, waits for them, and re-layouts: 13.7 us -> 3.13 us
    unnamed x3 -> x0, other arithmetic: 3.95 us -> none
where the time goes in v2:
time: 206 us
  Pallas kernels  203 us (99%)
  local copies, waits for them, and re-layouts  3.13 us (2%)
    pallas_call x1, Pallas kernels, body(): pl.pallas_call(functools.partial(kernel, nz), out_shape=jax.ShapeDtypeStr...  203 us

profile of v2, /device:TPU:249, one launch (start us, length us, event | category | flops | bytes accessed | tf_op | source)
XLA Modules:
  0.0 206.0 jit_solution(17699567714871022127)
XLA Ops:
  0.0 202.8 %shard_map.91 = bf16[1,2,128,4096]{3,2,1,0:T(8,128)(2,1)} custom-call(bf16[2,128,4096]{2,1,0:T(8,128)(2,1)} %stream_ref.1, s32[2,128]{1,0:T(2,128)} %ids_ref.1, bf16[1,576,4096]{2,1,0:T(8,128)(2,1)} %bitcast.1, f32[1,4,4096]{2,1,0:T(4,128)} %convw_ref.1, f32[1,4096]{1,0:T(1,128)} %convb_ref.1, f32[1,64]{1,0:T(1,128)} %decay_ref.1, f32[1,64]{1,0:T(1,128)} %stepb_ref.1, ...), custom_call_target="tpu_custom_call" | custom-call | tf_op jit(solution)/shard_map/pallas_call | solution.py:683
  202.8 3.1 %copy.11 = bf16[1,2,128,4096]{3,2,1,0:T(8,128)(2,1)} copy(bf16[1,2,128,4096]{3,2,1,0:T(8,128)(2,1)} %shard_map.91) | data formatting | bytes 4194304

commit v3 on v2

--- a/solution.py
+++ b/solution.py
@@ -354,22 +354,13 @@
     def wait_square(lx):
         wait_bytes(sm.at[lx, pl.ds(0, 3)], yr.at[lx, 3])
 
-    def push_rows(lx, kind, outbuf, inbuf, soutbuf, sinbuf):
+    def push(lx, kind, outbuf, inbuf):
         for dy in (2, 1, 3):
             yd = (y + dy) % NY
             remote(
                 outbuf.at[lx, yd], inbuf.at[lx, y], ys.at[lx, kind], yr.at[lx, kind], yd * NC + c, seg
             ).start()
-        for dy in (2, 1, 3):
-            yd = (y + dy) % NY
-            remote(
-                soutbuf.at[lx, yd],
-                sinbuf.at[lx, y],
-                ys.at[lx, kind + 1],
-                yr.at[lx, kind + 1],
-                yd * NC + c,
-                seg,
-            ).start()
+        inbuf[lx, y] = outbuf[lx, y]
 
     def conv_rows(l, r0, n):
         for j in range(NCH):
@@ -381,21 +372,13 @@
             inp[pl.ds(r0, n), cj] = (acc * (1.0 / (1.0 + jnp.exp(-acc)))).astype(BF16)
 
     def layer(l, carry):
-        @pl.when(phase == l + 3)
-        def _():
-            send_params()
-            send_weights()
-
         @pl.when((l == 0) & (phase > 0))
         def _():
-            wait_bytes(bcu.at[0, 0], yr.at[0, 0])
             wait_bytes(su.at[0, 0], yr.at[0, 1])
 
         @pl.when(l > 0)
         def _():
-            wait_bytes(bcu.at[l, pl.ds(0, 3)], yr.at[l, 0])
             wait_bytes(su.at[l, pl.ds(0, 3)], yr.at[l, 1])
-            wait_bytes(bcm.at[l, pl.ds(0, 3)], yr.at[l, 2])
             wait_square(l)
 
         inv8 = total_square(l)
@@ -408,23 +391,12 @@
                 ubuf.at[l + 1, pl.ds(T - 16, 16), :], halo.at[l], hs.at[l], hr.at[l], phase, seg + 1
             ).start()
 
-        @pl.when(l > 0)
-        def _():
-            send_out(l)
+        weights_2(l + 1)
 
         @pl.when(phase != l)
         def _():
             wait_bytes(ppb.at[l], wr.at[l, 6])
 
-        bc_u = (
-            bcu[l, 0].astype(F32) + bcu[l, 1].astype(F32) + bcu[l, 2].astype(F32) + bcu[l, 3].astype(F32)
-        )
-        bc_m = (
-            bcm[l, 0].astype(F32) + bcm[l, 1].astype(F32) + bcm[l, 2].astype(F32) + bcm[l, 3].astype(F32)
-        )
-        bc = (bc_u + inv8[0:1] * bc_m).astype(BF16)
-        bt = bc[0:64].astype(F32)
-        cs = jnp.transpose(bc[64:128].astype(F32)).astype(BF16)
         s_u = su[l, 0] + su[l, 1] + su[l, 2] + su[l, 3]
         s_m = sm[l, 0, 0:16] + sm[l, 1, 0:16] + sm[l, 2, 0:16] + sm[l, 3, 0:16]
         pre = s_u + inv8[0:1] * s_m + ppb[l, 72:88]
@@ -445,20 +417,28 @@
             xd = (x + d) % NX
             remote(gout.at[l], grecv.at[l, x], xs.at[l, 1], xr.at[l, 1], phase, z * NX + xd).start()
 
+        conv_rows(l, 16, T - 16)
+
+        @pl.when((l == 0) & (phase > 0))
+        def _():
+            wait_bytes(bcu.at[0, 0], yr.at[0, 0])
+
+        @pl.when(l > 0)
+        def _():
+            wait_bytes(bcu.at[l, pl.ds(0, 3)], yr.at[l, 0])
+            wait_bytes(bcm.at[l, pl.ds(0, 3)], yr.at[l, 2])
+
+        bc_u = (
+            bcu[l, 0].astype(F32) + bcu[l, 1].astype(F32) + bcu[l, 2].astype(F32) + bcu[l, 3].astype(F32)
+        )
+        bc_m = (
+            bcm[l, 0].astype(F32) + bcm[l, 1].astype(F32) + bcm[l, 2].astype(F32) + bcm[l, 3].astype(F32)
+        )
+        bc = (bc_u + inv8[0:1] * bc_m).astype(BF16)
+        bt = bc[0:64].astype(F32)
+        cs = jnp.transpose(bc[64:128].astype(F32)).astype(BF16)
         scores = jnp.dot(cs, bc[0:64], preferred_element_type=F32)
         scores = scores * msk[0]
-        cols = jnp.transpose(jnp.concatenate([run, cgain, jnp.zeros((T - 2 * PER, T), F32)], axis=0))
-        for j in range(NCH):
-            for i in range(2):
-                h = 2 * j + i
-                gap = jnp.broadcast_to(cols[:, h : h + 1], (T, T)) - run[h : h + 1]
-                w = scores * (jnp.exp(jnp.minimum(gap, 0.0)) * step[h : h + 1])
-                wts[j, :, pl.ds(128 * i, 128)] = w.astype(BF16)
-            g0 = jnp.broadcast_to(cols[:, PER + 2 * j : PER + 2 * j + 1], (T, T))
-            g1 = jnp.broadcast_to(cols[:, PER + 2 * j + 1 : PER + 2 * j + 2], (T, T))
-            gx[:, pl.ds(128 * j, 128)] = jnp.where(low, g0, g1)
-
-        conv_rows(l, 16, T - 16)
 
         @pl.when(seg > 0)
         def _():
@@ -486,9 +466,22 @@
             ).start()
         lrecv[l, x] = lout[l, x]
 
-        @pl.when(l == 0)
-        def _():
-            weights_2(1)
+        @pl.when(l > 0)
+        def _():
+            send_out(l)
+
+        @pl.when(phase == l + 3)
+        def _():
+            send_params()
+            send_weights()
+
+        cols = jnp.transpose(jnp.concatenate([run, cgain, jnp.zeros((T - 2 * PER, T), F32)], axis=0))
+        for j in range(NCH):
+            for i in range(2):
+                h = 2 * j + i
+                gap = jnp.broadcast_to(cols[:, h : h + 1], (T, T)) - run[h : h + 1]
+                w = scores * (jnp.exp(jnp.minimum(gap, 0.0)) * step[h : h + 1])
+                wts[j, :, pl.ds(128 * i, 128)] = w.astype(BF16)
 
         for j in range(NCH):
             cj = pl.ds(128 * j, 128)
@@ -517,7 +510,7 @@
             rb[1, :, cj] = r2
             rb[2, :, cj] = r3
             tout[l, :, cj] = rt.astype(BF16)
-        for d in range(REACH, 0, -1):
+        for d in range(1, REACH + 1):
 
             @pl.when(z + d < nz)
             def _(d=d):
@@ -531,15 +524,13 @@
 
         @pl.when(n < LAYERS)
         def _():
-            weights_1(n + 1)
             weights_3(n)
             a = product(wbuf[l], ubuf[l + 1])
             for g in range(GROUPS):
                 bcuo[n, g] = rows_of(a, g)
                 suo[n, g] = a[512 + 16 * g : 528 + 16 * g]
-            bcu[n, y] = bcuo[n, y]
-            su[n, y] = suo[n, y]
-            push_rows(n, 0, bcuo, bcu, suo, su)
+            push(n, 1, suo, su)
+            push(n, 0, bcuo, bcu)
 
         for d in range(1, REACH + 1):
 
@@ -569,7 +560,12 @@
             ).start()
         ent[l, x] = eout[l, x]
 
+        for j in range(NCH):
+            g0 = jnp.broadcast_to(cols[:, PER + 2 * j : PER + 2 * j + 1], (T, T))
+            g1 = jnp.broadcast_to(cols[:, PER + 2 * j + 1 : PER + 2 * j + 2], (T, T))
+            gx[:, pl.ds(128 * j, 128)] = jnp.where(low, g0, g1)
         wait_bytes(ent.at[l, pl.ds(0, 3)], xr.at[l, 2])
+        weights_1(n + 1)
         sq = jnp.zeros((T, 128), F32)
         for j in range(NCH):
             cj = pl.ds(128 * j, 128)
@@ -585,26 +581,22 @@
 
         @pl.when(n < LAYERS)
         def _():
-            a = product(wbuf[l], gmb[...])
+            v = gmb[...]
+            a = product(wbuf[l, 512:576, :], v)
+            for g in range(GROUPS):
+                smo[n, g, 0:16] = a[16 * g : 16 * g + 16]
+            push(n, 3, smo, sm)
+            a = product(wbuf[l, 0:512, :], v)
             for g in range(GROUPS):
                 bcmo[n, g] = rows_of(a, g)
-                smo[n, g, 0:16] = a[512 + 16 * g : 528 + 16 * g]
-            bcm[n, y] = bcmo[n, y]
-            sm[n, y] = smo[n, y]
-            push_rows(n, 2, bcmo, bcm, smo, sm)
+            push(n, 2, bcmo, bcm)
 
         @pl.when(n == LAYERS)
         def _():
             for g in range(GROUPS):
                 smo[n, g, 0:16] = jnp.zeros((16, 128), F32)
-            sm[n, y] = smo[n, y]
-            for dy in (2, 1, 3):
-                yd = (y + dy) % NY
-                remote(
-                    smo.at[n, yd], sm.at[n, y], ys.at[n, 3], yr.at[n, 3], yd * NC + c, seg
-                ).start()
-
-        weights_2(n + 1)
+            push(n, 3, smo, sm)
+
         return carry
 
     lax.fori_loop(0, LAYERS, layer, 0)

time: 206 us -> 200 us (0.971)
  Pallas kernels: 203 us -> 197 us
    pallas_call x1, Pallas kernels: 203 us -> 197 us  [body(): pl.pallas_call(functools.partial(kernel, nz), out_shape=jax.ShapeDtypeStr...]
where the time goes in v3:
time: 200 us
  Pallas kernels  197 us (98%)
  local copies, waits for them, and re-layouts  3.13 us (2%)
    pallas_call x1, Pallas kernels, body(): pl.pallas_call(functools.partial(kernel, nz), out_shape=jax.ShapeDtypeStr...  197 us

profile of v3, /device:TPU:249, one launch (start us, length us, event | category | flops | bytes accessed | tf_op | source)
XLA Modules:
  0.0 199.9 jit_solution(4365893759902361444)
XLA Ops:
  0.0 196.8 %shard_map.91 = bf16[1,2,128,4096]{3,2,1,0:T(8,128)(2,1)} custom-call(bf16[2,128,4096]{2,1,0:T(8,128)(2,1)} %stream_ref.1, s32[2,128]{1,0:T(2,128)} %ids_ref.1, bf16[1,576,4096]{2,1,0:T(8,128)(2,1)} %bitcast.1, f32[1,4,4096]{2,1,0:T(4,128)} %convw_ref.1, f32[1,4096]{1,0:T(1,128)} %convb_ref.1, f32[1,64]{1,0:T(1,128)} %decay_ref.1, f32[1,64]{1,0:T(1,128)} %stepb_ref.1, ...), custom_call_target="tpu_custom_call" | custom-call | tf_op jit(solution)/shard_map/pallas_call | solution.py:675
  196.8 3.1 %copy.11 = bf16[1,2,128,4096]{3,2,1,0:T(8,128)(2,1)} copy(bf16[1,2,128,4096]{3,2,1,0:T(8,128)(2,1)} %shard_map.91) | data formatting | bytes 4194304

commit v4 on v3

--- a/solution.py
+++ b/solution.py
@@ -64,9 +64,11 @@
     inp,
     wts,
     bcu,
-    bcm,
+    bm,
+    cm,
     bcuo,
-    bcmo,
+    bmo,
+    cmo,
     su,
     sm,
     suo,
@@ -249,6 +251,7 @@
             whole = wbuf.at[n - 1]
             remote(whole, whole, wrs.at[n], wr.at[n, 5], y * NC + 1 - c, seg).start()
 
+    def weights_4(n):
         @pl.when((n < LAYERS) & (c != n % NC))
         def _():
             wait_bytes(wbuf.at[n - 1], wr.at[n, 5])
@@ -269,17 +272,16 @@
         send_params()
         cp_w0.wait()
         cp_s0.wait()
-        both = strm[...].reshape(MICRO * T, CH * GROUPS)
-        for r in range(4):
-            rr = pl.ds(WPART * r, WPART)
-            p0[rr, :] = product(w0[rr, :], both)
         for m in range(MICRO):
             at = LAYERS * m
-            cm = pl.ds(T * m, T)
+            mine = strm[m]
+            for r in range(4):
+                rr = pl.ds(WPART * r, WPART)
+                p0[rr, :] = product(w0[rr, :], mine)
             for g in range(GROUPS):
-                bcuo[at, g, 0:64] = p0[pl.ds(64 * g, 64), cm].astype(BF16)
-                bcuo[at, g, 64:128] = p0[pl.ds(256 + 64 * g, 64), cm].astype(BF16)
-                suo[at, g] = p0[pl.ds(512 + 16 * g, 16), cm]
+                bcuo[at, g, 0:64] = p0[pl.ds(64 * g, 64), :].astype(BF16)
+                bcuo[at, g, 64:128] = p0[pl.ds(256 + 64 * g, 64), :].astype(BF16)
+                suo[at, g] = p0[pl.ds(512 + 16 * g, 16), :]
             for g in (2, 1, 3, 0):
                 p = g * NC + m
                 if p > 0:
@@ -288,7 +290,7 @@
         bcu[0, 0] = bcuo[0, 0]
         su[0, 0] = suo[0, 0]
 
-    @pl.when((phase == 1) | (phase == 2))
+    @pl.when((phase >= 1) & (phase <= 3))
     def _():
         send_params()
         send_weights()
@@ -299,7 +301,8 @@
     def _():
         pltpu.make_async_copy(quarter(y), wbuf.at[phase - 1], loc.at[2]).wait()
 
-    bcm[0] = jnp.zeros((NY, T, 128), BF16)
+    bm[0] = jnp.zeros((NY, 64, 128), BF16)
+    cm[0] = jnp.zeros((NY, 64, 128), BF16)
     sm[0] = jnp.zeros((NY, 24, 128), F32)
     for s in range(1, NY):
         bcu[0, s] = jnp.zeros((T, 128), BF16)
@@ -327,6 +330,7 @@
     sg[1, 8:16] = jnp.where(own_row == own_last, 1.0, 0.0)
     sum_up = jnp.where(t_at <= lane, 1.0, 0.0)
     weights_1(1)
+    weights_1(2)
 
     def total_square(lx):
         s = sm[lx, 0, 16:24] + sm[lx, 1, 16:24] + sm[lx, 2, 16:24] + sm[lx, 3, 16:24]
@@ -391,7 +395,11 @@
                 ubuf.at[l + 1, pl.ds(T - 16, 16), :], halo.at[l], hs.at[l], hr.at[l], phase, seg + 1
             ).start()
 
-        weights_2(l + 1)
+        @pl.when(l == 0)
+        def _():
+            weights_2(1)
+
+        weights_2(l + 2)
 
         @pl.when(phase != l)
         def _():
@@ -426,19 +434,16 @@
         @pl.when(l > 0)
         def _():
             wait_bytes(bcu.at[l, pl.ds(0, 3)], yr.at[l, 0])
-            wait_bytes(bcm.at[l, pl.ds(0, 3)], yr.at[l, 2])
-
-        bc_u = (
-            bcu[l, 0].astype(F32) + bcu[l, 1].astype(F32) + bcu[l, 2].astype(F32) + bcu[l, 3].astype(F32)
-        )
-        bc_m = (
-            bcm[l, 0].astype(F32) + bcm[l, 1].astype(F32) + bcm[l, 2].astype(F32) + bcm[l, 3].astype(F32)
-        )
-        bc = (bc_u + inv8[0:1] * bc_m).astype(BF16)
-        bt = bc[0:64].astype(F32)
-        cs = jnp.transpose(bc[64:128].astype(F32)).astype(BF16)
-        scores = jnp.dot(cs, bc[0:64], preferred_element_type=F32)
-        scores = scores * msk[0]
+            wait_bytes(bm.at[l, pl.ds(0, 3)], yr.at[l, 2])
+
+        def summed(ref, r0):
+            r = pl.ds(r0, 64)
+            return (ref[l, 0, r].astype(F32) + ref[l, 1, r].astype(F32)) + (
+                ref[l, 2, r].astype(F32) + ref[l, 3, r].astype(F32)
+            )
+
+        b_cols = (summed(bcu, 0) + inv8[0:1] * summed(bm, 0)).astype(BF16)
+        bt = b_cols.astype(F32)
 
         @pl.when(seg > 0)
         def _():
@@ -470,11 +475,19 @@
         def _():
             send_out(l)
 
-        @pl.when(phase == l + 3)
+        @pl.when(phase == l + 4)
         def _():
             send_params()
             send_weights()
 
+        @pl.when(l > 0)
+        def _():
+            wait_bytes(cm.at[l, pl.ds(0, 3)], yr.at[l, 4])
+
+        c_cols = (summed(bcu, 64) + inv8[0:1] * summed(cm, 0)).astype(BF16)
+        cs = jnp.transpose(c_cols.astype(F32)).astype(BF16)
+        scores = jnp.dot(cs, b_cols, preferred_element_type=F32)
+        scores = scores * msk[0]
         cols = jnp.transpose(jnp.concatenate([run, cgain, jnp.zeros((T - 2 * PER, T), F32)], axis=0))
         for j in range(NCH):
             for i in range(2):
@@ -524,7 +537,11 @@
 
         @pl.when(n < LAYERS)
         def _():
-            weights_3(n)
+            @pl.when(l == 0)
+            def _():
+                weights_3(n)
+
+            weights_4(n)
             a = product(wbuf[l], ubuf[l + 1])
             for g in range(GROUPS):
                 bcuo[n, g] = rows_of(a, g)
@@ -565,7 +582,7 @@
             g1 = jnp.broadcast_to(cols[:, PER + 2 * j + 1 : PER + 2 * j + 2], (T, T))
             gx[:, pl.ds(128 * j, 128)] = jnp.where(low, g0, g1)
         wait_bytes(ent.at[l, pl.ds(0, 3)], xr.at[l, 2])
-        weights_1(n + 1)
+        weights_1(n + 2)
         sq = jnp.zeros((T, 128), F32)
         for j in range(NCH):
             cj = pl.ds(128 * j, 128)
@@ -586,10 +603,14 @@
             for g in range(GROUPS):
                 smo[n, g, 0:16] = a[16 * g : 16 * g + 16]
             push(n, 3, smo, sm)
-            a = product(wbuf[l, 0:512, :], v)
+            a = product(wbuf[l, 0:256, :], v).astype(BF16)
             for g in range(GROUPS):
-                bcmo[n, g] = rows_of(a, g)
-            push(n, 2, bcmo, bcm)
+                bmo[n, g] = a[64 * g : 64 * g + 64]
+            push(n, 2, bmo, bm)
+            a = product(wbuf[l, 256:512, :], v).astype(BF16)
+            for g in range(GROUPS):
+                cmo[n, g] = a[64 * g : 64 * g + 64]
+            push(n, 4, cmo, cm)
 
         @pl.when(n == LAYERS)
         def _():
@@ -597,6 +618,7 @@
                 smo[n, g, 0:16] = jnp.zeros((16, 128), F32)
             push(n, 3, smo, sm)
 
+        weights_3(n + 1)
         return carry
 
     lax.fori_loop(0, LAYERS, layer, 0)
@@ -613,7 +635,8 @@
         def _():
             wait_bytes(bcuo.at[n, pl.ds(0, 3)], ys.at[n, 0])
             wait_bytes(suo.at[n, pl.ds(0, 3)], ys.at[n, 1])
-            wait_bytes(bcmo.at[n, pl.ds(0, 3)], ys.at[n, 2])
+            wait_bytes(bmo.at[n, pl.ds(0, 3)], ys.at[n, 2])
+            wait_bytes(cmo.at[n, pl.ds(0, 3)], ys.at[n, 4])
 
         wait_bytes(smo.at[n, pl.ds(0, 3)], ys.at[n, 3])
         wait_bytes(ubuf.at[n + 1], outs.at[n])
@@ -691,7 +714,7 @@
             vmem((T, CH), BF16),
             vmem((GROUPS, 88, 128), F32),
             vmem((HEADS, 128), F32),
-            vmem((PROJ, MICRO * T), F32),
+            vmem((PROJ, T), F32),
             vmem((LAYERS, 88, 128), F32),
             vmem((8, T), jnp.int32),
             vmem((8, T), jnp.int32),
@@ -701,9 +724,11 @@
             vmem((T, CH), BF16),
             vmem((NCH, T, 256), BF16),
             vmem((n1, NY, T, 128), BF16),
+            vmem((n1, NY, 64, 128), BF16),
+            vmem((n1, NY, 64, 128), BF16),
             vmem((n1, NY, T, 128), BF16),
-            vmem((n1, NY, T, 128), BF16),
-            vmem((n1, NY, T, 128), BF16),
+            vmem((n1, NY, 64, 128), BF16),
+            vmem((n1, NY, 64, 128), BF16),
             vmem((n1, NY, 16, 128), F32),
             vmem((n1, NY, 24, 128), F32),
             vmem((n1, NY, 16, 128), F32),
@@ -722,8 +747,8 @@
             vmem((LAYERS, NX, 16, CH), BF16),
             vmem((T, CH), F32),
             vmem((T, CH), F32),
-            dma((n1, 4)),
-            dma((n1, 4)),
+            dma((n1, 5)),
+            dma((n1, 5)),
             dma((NY * NC, 2)),
             dma((LAYERS, 3)),
             dma((LAYERS, 3)),

time: 200 us -> 204 us (1.020)
  Pallas kernels: 197 us -> 200 us
    pallas_call x1, Pallas kernels: 197 us -> 200 us  [body(): pl.pallas_call(functools.partial(kernel, nz), out_shape=jax.ShapeDtypeStr...]
where the time goes in v4:
time: 204 us
  Pallas kernels  200 us (98%)
  local copies, waits for them, and re-layouts  3.13 us (2%)
    pallas_call x1, Pallas kernels, body(): pl.pallas_call(functools.partial(kernel, nz), out_shape=jax.ShapeDtypeStr...  200 us

profile of v4, /device:TPU:249, one launch (start us, length us, event | category | flops | bytes accessed | tf_op | source)
XLA Modules:
  0.0 203.6 jit_solution(4027837523795130909)
XLA Ops:
  0.0 200.4 %shard_map.91 = bf16[1,2,128,4096]{3,2,1,0:T(8,128)(2,1)} custom-call(bf16[2,128,4096]{2,1,0:T(8,128)(2,1)} %stream_ref.1, s32[2,128]{1,0:T(2,128)} %ids_ref.1, bf16[1,576,4096]{2,1,0:T(8,128)(2,1)} %bitcast.1, f32[1,4,4096]{2,1,0:T(4,128)} %convw_ref.1, f32[1,4096]{1,0:T(1,128)} %convb_ref.1, f32[1,64]{1,0:T(1,128)} %decay_ref.1, f32[1,64]{1,0:T(1,128)} %stepb_ref.1, ...), custom_call_target="tpu_custom_call" | custom-call | tf_op jit(solution)/shard_map/pallas_call | solution.py:698
  200.5 3.1 %copy.11 = bf16[1,2,128,4096]{3,2,1,0:T(8,128)(2,1)} copy(bf16[1,2,128,4096]{3,2,1,0:T(8,128)(2,1)} %shard_map.91) | data formatting | bytes 4194304

commit v5 on v4

--- a/solution.py
+++ b/solution.py
@@ -202,7 +202,7 @@
             p = (phase + d) % (NY * NC)
             remote(pps.at[p // NC], ppb.at[phase], ppsem.at[p], wr.at[phase, 6], p, seg).start()
 
-    def part(n, i, r0, rows):
+    def piece(n, i, r0, rows):
         return wbuf.at[n - 1, pl.ds(pl.multiple_of(i * WPART + r0, 16), rows), :]
 
     def send_weights():
@@ -211,7 +211,7 @@
             yd = (y + dy) % NY
             remote(
                 proj_ref.at[0, rows, pl.ds(pl.multiple_of(yd * CH, CH), CH)],
-                part(phase, x, 0, WPART),
+                piece(phase, x, 0, WPART),
                 wss.at[yd],
                 wr.at[phase, 0],
                 yd * NC + c,
@@ -228,7 +228,7 @@
     def weights_1(n):
         @pl.when(relays(n))
         def _():
-            mine = part(n, x, 0, WPART)
+            mine = piece(n, x, 0, WPART)
             wait_bytes(mine, wr.at[n, 0])
             remote(mine, mine, wxs.at[n, 0], wr.at[n, 1], phase, right).start()
             remote(mine, mine, wxs.at[n, 1], wr.at[n, 2], phase, left).start()
@@ -236,18 +236,18 @@
     def weights_2(n):
         @pl.when(relays(n))
         def _():
-            wait_bytes(part(n, x, 0, WPART), wr.at[n, 1])
-            first = part(n, (x + NX - 1) % NX, 0, WHALF)
+            wait_bytes(piece(n, x, 0, WPART), wr.at[n, 1])
+            first = piece(n, (x + NX - 1) % NX, 0, WHALF)
             remote(first, first, wxs.at[n, 2], wr.at[n, 3], phase, right).start()
-            wait_bytes(part(n, x, 0, WPART), wr.at[n, 2])
-            last = part(n, (x + 1) % NX, WHALF, WPART - WHALF)
+            wait_bytes(piece(n, x, 0, WPART), wr.at[n, 2])
+            last = piece(n, (x + 1) % NX, WHALF, WPART - WHALF)
             remote(last, last, wxs.at[n, 3], wr.at[n, 4], phase, left).start()
 
     def weights_3(n):
         @pl.when(relays(n))
         def _():
-            wait_bytes(part(n, x, 0, WHALF), wr.at[n, 3])
-            wait_bytes(part(n, x, 0, WPART - WHALF), wr.at[n, 4])
+            wait_bytes(piece(n, x, 0, WHALF), wr.at[n, 3])
+            wait_bytes(piece(n, x, 0, WPART - WHALF), wr.at[n, 4])
             whole = wbuf.at[n - 1]
             remote(whole, whole, wrs.at[n], wr.at[n, 5], y * NC + 1 - c, seg).start()
 
@@ -330,7 +330,6 @@
     sg[1, 8:16] = jnp.where(own_row == own_last, 1.0, 0.0)
     sum_up = jnp.where(t_at <= lane, 1.0, 0.0)
     weights_1(1)
-    weights_1(2)
 
     def total_square(lx):
         s = sm[lx, 0, 16:24] + sm[lx, 1, 16:24] + sm[lx, 2, 16:24] + sm[lx, 3, 16:24]
@@ -395,11 +394,9 @@
                 ubuf.at[l + 1, pl.ds(T - 16, 16), :], halo.at[l], hs.at[l], hr.at[l], phase, seg + 1
             ).start()
 
-        @pl.when(l == 0)
-        def _():
-            weights_2(1)
-
-        weights_2(l + 2)
+        @pl.when(l > 0)
+        def _():
+            weights_3(l + 1)
 
         @pl.when(phase != l)
         def _():
@@ -423,7 +420,7 @@
         grecv[l, x] = gain8
         for d in range(1, NX):
             xd = (x + d) % NX
-            remote(gout.at[l], grecv.at[l, x], xs.at[l, 1], xr.at[l, 1], phase, z * NX + xd).start()
+            remote(gout.at[l], grecv.at[l, x], xs.at[l, 4], xr.at[l, 4], phase, z * NX + xd).start()
 
         conv_rows(l, 16, T - 16)
 
@@ -457,19 +454,25 @@
         conv_rows(l, 0, 16)
 
         low64 = low[0:64]
-        for j in range(NCH):
-            cj = pl.ds(128 * j, 128)
-            left = jnp.concatenate([bt * tail[2 * j : 2 * j + 1], bt * tail[2 * j + 1 : 2 * j + 2]], axis=0)
-            both = jnp.dot(left.astype(BF16), inp[:, cj], preferred_element_type=F32)
-            st = jnp.where(low64, both[0:64], both[64:128]).astype(BF16)
-            for q in range(NX):
-                lout[l, q, :, cj] = st[16 * q : 16 * q + 16]
-        for d in (2, 1, 3):
-            xd = (x + d) % NX
-            remote(
-                lout.at[l, xd], lrecv.at[l, x], xs.at[l, 0], xr.at[l, 0], phase, z * NX + xd
-            ).start()
-        lrecv[l, x] = lout[l, x]
+        for half in range(2):
+            for j in range(4 * half, 4 * half + 4):
+                ch = pl.ds(128 * (j % 4), 128)
+                left = jnp.concatenate([bt * tail[2 * j : 2 * j + 1], bt * tail[2 * j + 1 : 2 * j + 2]], axis=0)
+                both = jnp.dot(left.astype(BF16), inp[:, pl.ds(128 * j, 128)], preferred_element_type=F32)
+                st = jnp.where(low64, both[0:64], both[64:128]).astype(BF16)
+                for q in range(NX):
+                    lout[l, half, q, :, ch] = st[16 * q : 16 * q + 16]
+            for d in (2, 1, 3):
+                xd = (x + d) % NX
+                remote(
+                    lout.at[l, half, xd],
+                    lrecv.at[l, half, x],
+                    xs.at[l, half],
+                    xr.at[l, half],
+                    phase,
+                    z * NX + xd,
+                ).start()
+            lrecv[l, half, x] = lout[l, half, x]
 
         @pl.when(l > 0)
         def _():
@@ -479,6 +482,11 @@
         def _():
             send_params()
             send_weights()
+
+        @pl.when(l == 0)
+        def _():
+            weights_2(1)
+            weights_1(2)
 
         @pl.when(l > 0)
         def _():
@@ -504,8 +512,7 @@
             intra = jnp.dot(wts[j], right, preferred_element_type=F32)
             m0[:, cj] = intra + ppb[l, pl.ds(48 + j, 1), :] * vf
 
-        wait_bytes(grecv.at[l, pl.ds(0, 3)], xr.at[l, 1])
-        wait_bytes(lrecv.at[l, pl.ds(0, 3)], xr.at[l, 0])
+        wait_bytes(grecv.at[l, pl.ds(0, 3)], xr.at[l, 4])
         p1 = grecv[l, 0]
         p2 = p1 * grecv[l, 1]
         p3 = p2 * grecv[l, 2]
@@ -513,27 +520,74 @@
         ga = grecv[l, 1]
         gb = grecv[l, 2]
         gc = grecv[l, 3]
-        for j in range(NCH):
-            cj = pl.ds(128 * j, 128)
-            r1 = lrecv[l, 0, :, cj].astype(F32)
-            r2 = lrecv[l, 1, :, cj].astype(F32) + ga[j : j + 1] * r1
-            r3 = lrecv[l, 2, :, cj].astype(F32) + gb[j : j + 1] * r2
-            rt = lrecv[l, 3, :, cj].astype(F32) + gc[j : j + 1] * r3
-            rb[0, :, cj] = r1
-            rb[1, :, cj] = r2
-            rb[2, :, cj] = r3
-            tout[l, :, cj] = rt.astype(BF16)
-        for d in range(1, REACH + 1):
-
-            @pl.when(z + d < nz)
-            def _(d=d):
-                to = (z + d) * NX + x
+        n = l + 1
+        for half in range(2):
+            wait_bytes(lrecv.at[l, half, pl.ds(0, 3)], xr.at[l, half])
+            for j in range(4 * half, 4 * half + 4):
+                cj = pl.ds(128 * j, 128)
+                ch = pl.ds(128 * (j % 4), 128)
+                r1 = lrecv[l, half, 0, :, ch].astype(F32)
+                r2 = lrecv[l, half, 1, :, ch].astype(F32) + ga[j : j + 1] * r1
+                r3 = lrecv[l, half, 2, :, ch].astype(F32) + gb[j : j + 1] * r2
+                rt = lrecv[l, half, 3, :, ch].astype(F32) + gc[j : j + 1] * r3
+                rb[0, :, cj] = r1
+                rb[1, :, cj] = r2
+                rb[2, :, cj] = r3
+                tout[l, half, :, ch] = rt.astype(BF16)
+            for d in range(1, REACH + 1):
+
+                @pl.when(z + d < nz)
+                def _(d=d, half=half):
+                    to = (z + d) * NX + x
+                    if half == 0:
+                        remote(
+                            ggout.at[l], ggrecv.at[l, d - 1], zs.at[l, 2, d - 1], zr.at[l, 2, d - 1], phase, to
+                        ).start()
+                    remote(
+                        tout.at[l, half],
+                        trecv.at[l, half, d - 1],
+                        zs.at[l, half, d - 1],
+                        zr.at[l, half, d - 1],
+                        phase,
+                        to,
+                    ).start()
+
+            for d in range(1, REACH + 1):
+
+                @pl.when(z >= d)
+                def _(d=d, half=half):
+                    if half == 0:
+                        wait_bytes(ggrecv.at[l, d - 1], zr.at[l, 2, d - 1])
+                    wait_bytes(trecv.at[l, half, d - 1], zr.at[l, half, d - 1])
+
+                @pl.when(z < d)
+                def _(d=d, half=half):
+                    if half == 0:
+                        ggrecv[l, d - 1] = jnp.zeros((8, 128), F32)
+                    trecv[l, half, d - 1] = jnp.zeros((16, CH // 2), BF16)
+
+            for j in range(4 * half, 4 * half + 4):
+                cj = pl.ds(128 * j, 128)
+                ch = pl.ds(128 * (j % 4), 128)
+                e = trecv[l, half, 3, :, ch].astype(F32)
+                for d in (2, 1, 0):
+                    e = trecv[l, half, d, :, ch].astype(F32) + ggrecv[l, d, pl.ds(j, 1), :] * e
+                eout[l, half, 0, :, ch] = e.astype(BF16)
+                eout[l, half, 1, :, ch] = (rb[0, :, cj] + p1[j : j + 1] * e).astype(BF16)
+                eout[l, half, 2, :, ch] = (rb[1, :, cj] + p2[j : j + 1] * e).astype(BF16)
+                eout[l, half, 3, :, ch] = (rb[2, :, cj] + p3[j : j + 1] * e).astype(BF16)
+            for d in (2, 1, 3):
+                xd = (x + d) % NX
                 remote(
-                    ggout.at[l], ggrecv.at[l, d - 1], zs.at[l, REACH + d - 1], zr.at[l, REACH + d - 1], phase, to
+                    eout.at[l, half, xd],
+                    ent.at[l, half, x],
+                    xs.at[l, 2 + half],
+                    xr.at[l, 2 + half],
+                    phase,
+                    z * NX + xd,
                 ).start()
-                remote(tout.at[l], trecv.at[l, d - 1], zs.at[l, d - 1], zr.at[l, d - 1], phase, to).start()
-
-        n = l + 1
+            ent[l, half, x] = eout[l, half, x]
+
 
         @pl.when(n < LAYERS)
         def _():
@@ -549,49 +603,25 @@
             push(n, 1, suo, su)
             push(n, 0, bcuo, bcu)
 
-        for d in range(1, REACH + 1):
-
-            @pl.when(z >= d)
-            def _(d=d):
-                wait_bytes(ggrecv.at[l, d - 1], zr.at[l, REACH + d - 1])
-                wait_bytes(trecv.at[l, d - 1], zr.at[l, d - 1])
-
-            @pl.when(z < d)
-            def _(d=d):
-                ggrecv[l, d - 1] = jnp.zeros((8, 128), F32)
-                trecv[l, d - 1] = jnp.zeros((16, CH), BF16)
-
-        for j in range(NCH):
-            cj = pl.ds(128 * j, 128)
-            e = trecv[l, 3, :, cj].astype(F32)
-            for d in (2, 1, 0):
-                e = trecv[l, d, :, cj].astype(F32) + ggrecv[l, d, pl.ds(j, 1), :] * e
-            eout[l, 0, :, cj] = e.astype(BF16)
-            eout[l, 1, :, cj] = (rb[0, :, cj] + p1[j : j + 1] * e).astype(BF16)
-            eout[l, 2, :, cj] = (rb[1, :, cj] + p2[j : j + 1] * e).astype(BF16)
-            eout[l, 3, :, cj] = (rb[2, :, cj] + p3[j : j + 1] * e).astype(BF16)
-        for d in (2, 1, 3):
-            xd = (x + d) % NX
-            remote(
-                eout.at[l, xd], ent.at[l, x], xs.at[l, 2], xr.at[l, 2], phase, z * NX + xd
-            ).start()
-        ent[l, x] = eout[l, x]
-
         for j in range(NCH):
             g0 = jnp.broadcast_to(cols[:, PER + 2 * j : PER + 2 * j + 1], (T, T))
             g1 = jnp.broadcast_to(cols[:, PER + 2 * j + 1 : PER + 2 * j + 2], (T, T))
             gx[:, pl.ds(128 * j, 128)] = jnp.where(low, g0, g1)
-        wait_bytes(ent.at[l, pl.ds(0, 3)], xr.at[l, 2])
-        weights_1(n + 2)
         sq = jnp.zeros((T, 128), F32)
-        for j in range(NCH):
-            cj = pl.ds(128 * j, 128)
-            part = jnp.dot(cs, ent[l, :, :, cj].reshape(STATE, 128), preferred_element_type=F32)
-            mixed = m0[:, cj] + part * gx[:, cj]
-            sq = sq + mixed * mixed
-            scaled = ppb[l, pl.ds(40 + j, 1), :] * mixed
-            gm[:, cj] = scaled
-            gmb[:, cj] = scaled.astype(BF16)
+        for half in range(2):
+            wait_bytes(ent.at[l, half, pl.ds(0, 3)], xr.at[l, 2 + half])
+            if half == 1:
+                weights_2(n + 1)
+                weights_1(n + 2)
+            for j in range(4 * half, 4 * half + 4):
+                cj = pl.ds(128 * j, 128)
+                state = ent[l, half, :, :, pl.ds(128 * (j % 4), 128)].reshape(STATE, 128)
+                part = jnp.dot(cs, state, preferred_element_type=F32)
+                mixed = m0[:, cj] + part * gx[:, cj]
+                sq = sq + mixed * mixed
+                scaled = ppb[l, pl.ds(40 + j, 1), :] * mixed
+                gm[:, cj] = scaled
+                gmb[:, cj] = scaled.astype(BF16)
         sq_row = jnp.broadcast_to(jnp.sum(jnp.transpose(sq), axis=0, keepdims=True), (8, T))
         for g in range(GROUPS):
             smo[n, g, 16:24] = sq_row
@@ -618,7 +648,6 @@
                 smo[n, g, 0:16] = jnp.zeros((16, 128), F32)
             push(n, 3, smo, sm)
 
-        weights_3(n + 1)
         return carry
 
     lax.fori_loop(0, LAYERS, layer, 0)
@@ -640,15 +669,17 @@
 
         wait_bytes(smo.at[n, pl.ds(0, 3)], ys.at[n, 3])
         wait_bytes(ubuf.at[n + 1], outs.at[n])
-        wait_bytes(lout.at[l, pl.ds(0, 3)], xs.at[l, 0])
-        wait_bytes(grecv.at[l, pl.ds(0, 3)], xs.at[l, 1])
-        wait_bytes(eout.at[l, pl.ds(0, 3)], xs.at[l, 2])
+        wait_bytes(grecv.at[l, pl.ds(0, 3)], xs.at[l, 4])
+        for half in range(2):
+            wait_bytes(lout.at[l, half, pl.ds(0, 3)], xs.at[l, half])
+            wait_bytes(eout.at[l, half, pl.ds(0, 3)], xs.at[l, 2 + half])
         for d in range(1, REACH + 1):
 
             @pl.when(z + d < nz)
             def _(d=d):
-                wait_bytes(ggout.at[l], zs.at[l, REACH + d - 1])
-                wait_bytes(tout.at[l], zs.at[l, d - 1])
+                wait_bytes(ggout.at[l], zs.at[l, 2, d - 1])
+                for half in range(2):
+                    wait_bytes(tout.at[l, half], zs.at[l, half, d - 1])
 
         @pl.when(seg < nseg - 1)
         def _():
@@ -658,7 +689,7 @@
         def _():
             wait_bytes(wbuf.at[l], wrs.at[n])
             for i, rows in enumerate((WPART, WPART, WHALF, WPART - WHALF)):
-                wait_bytes(part(n, x, 0, rows), wxs.at[n, i])
+                wait_bytes(piece(n, x, 0, rows), wxs.at[n, i])
 
         @pl.when(phase != l)
         def _():
@@ -672,7 +703,7 @@
     @pl.when(phase > 0)
     def _():
         for dy in range(1, NY):
-            wait_bytes(part(1, x, 0, WPART), wss.at[(y + dy) % NY])
+            wait_bytes(piece(1, x, 0, WPART), wss.at[(y + dy) % NY])
         wait_bytes(wbuf.at[0], wss.at[y])
 
     @pl.when(phase == 0)
@@ -734,26 +765,26 @@
             vmem((n1, NY, 16, 128), F32),
             vmem((n1, NY, 24, 128), F32),
             vmem((2, 16, 128), F32),
-            vmem((LAYERS, NX, 16, CH), BF16),
-            vmem((LAYERS, NX, 16, CH), BF16),
+            vmem((LAYERS, 2, NX, 16, CH // 2), BF16),
+            vmem((LAYERS, 2, NX, 16, CH // 2), BF16),
             vmem((LAYERS, 8, 128), F32),
             vmem((LAYERS, NX, 8, 128), F32),
-            vmem((LAYERS, 16, CH), BF16),
+            vmem((LAYERS, 2, 16, CH // 2), BF16),
             vmem((LAYERS, 8, 128), F32),
-            vmem((LAYERS, REACH, 16, CH), BF16),
+            vmem((LAYERS, 2, REACH, 16, CH // 2), BF16),
             vmem((LAYERS, REACH, 8, 128), F32),
             vmem((3, 16, CH), F32),
-            vmem((LAYERS, NX, 16, CH), BF16),
-            vmem((LAYERS, NX, 16, CH), BF16),
+            vmem((LAYERS, 2, NX, 16, CH // 2), BF16),
+            vmem((LAYERS, 2, NX, 16, CH // 2), BF16),
             vmem((T, CH), F32),
             vmem((T, CH), F32),
             dma((n1, 5)),
             dma((n1, 5)),
             dma((NY * NC, 2)),
-            dma((LAYERS, 3)),
-            dma((LAYERS, 3)),
-            dma((LAYERS, 2 * REACH)),
-            dma((LAYERS, 2 * REACH)),
+            dma((LAYERS, 5)),
+            dma((LAYERS, 5)),
+            dma((LAYERS, 3, REACH)),
+            dma((LAYERS, 3, REACH)),
             dma((LAYERS,)),
             dma((LAYERS,)),
             dma((LAYERS, 7)),

time: 204 us -> 211 us (1.034)
  Pallas kernels: 200 us -> 208 us
    pallas_call x1, Pallas kernels: 200 us -> 208 us  [body(): pl.pallas_call(functools.partial(kernel, nz), out_shape=jax.ShapeDtypeStr...]
where the time goes in v5:
time: 211 us
  Pallas kernels  208 us (99%)
  local copies, waits for them, and re-layouts  3.13 us (1%)
    pallas_call x1, Pallas kernels, body(): pl.pallas_call(functools.partial(kernel, nz), out_shape=jax.ShapeDtypeStr...  208 us

profile of v5, /device:TPU:249, one launch (start us, length us, event | category | flops | bytes accessed | tf_op | source)
XLA Modules:
  0.0 210.9 jit_solution(16904212956412966457)
XLA Ops:
  0.0 207.7 %shard_map.91 = bf16[1,2,128,4096]{3,2,1,0:T(8,128)(2,1)} custom-call(bf16[2,128,4096]{2,1,0:T(8,128)(2,1)} %stream_ref.1, s32[2,128]{1,0:T(2,128)} %ids_ref.1, bf16[1,576,4096]{2,1,0:T(8,128)(2,1)} %bitcast.1, f32[1,4,4096]{2,1,0:T(4,128)} %convw_ref.1, f32[1,4096]{1,0:T(1,128)} %convb_ref.1, f32[1,64]{1,0:T(1,128)} %decay_ref.1, f32[1,64]{1,0:T(1,128)} %stepb_ref.1, ...), custom_call_target="tpu_custom_call" | custom-call | tf_op jit(solution)/shard_map/pallas_call | solution.py:729
  207.7 3.1 %copy.11 = bf16[1,2,128,4096]{3,2,1,0:T(8,128)(2,1)} copy(bf16[1,2,128,4096]{3,2,1,0:T(8,128)(2,1)} %shard_map.91) | data formatting | bytes 4194304

commit v6 on v3

--- a/solution.py
+++ b/solution.py
@@ -269,17 +269,16 @@
         send_params()
         cp_w0.wait()
         cp_s0.wait()
-        both = strm[...].reshape(MICRO * T, CH * GROUPS)
-        for r in range(4):
-            rr = pl.ds(WPART * r, WPART)
-            p0[rr, :] = product(w0[rr, :], both)
         for m in range(MICRO):
             at = LAYERS * m
-            cm = pl.ds(T * m, T)
+            mine = strm[m]
+            for r in range(4):
+                rr = pl.ds(WPART * r, WPART)
+                p0[rr, :] = product(w0[rr, :], mine)
             for g in range(GROUPS):
-                bcuo[at, g, 0:64] = p0[pl.ds(64 * g, 64), cm].astype(BF16)
-                bcuo[at, g, 64:128] = p0[pl.ds(256 + 64 * g, 64), cm].astype(BF16)
-                suo[at, g] = p0[pl.ds(512 + 16 * g, 16), cm]
+                bcuo[at, g, 0:64] = p0[pl.ds(64 * g, 64), :].astype(BF16)
+                bcuo[at, g, 64:128] = p0[pl.ds(256 + 64 * g, 64), :].astype(BF16)
+                suo[at, g] = p0[pl.ds(512 + 16 * g, 16), :]
             for g in (2, 1, 3, 0):
                 p = g * NC + m
                 if p > 0:
@@ -288,10 +287,10 @@
         bcu[0, 0] = bcuo[0, 0]
         su[0, 0] = suo[0, 0]
 
-    @pl.when((phase == 1) | (phase == 2))
-    def _():
+    @pl.when(phase == 1)
+    def _():
+        send_weights()
         send_params()
-        send_weights()
 
     cp_u.wait()
 
@@ -326,7 +325,6 @@
     sg[1, 0:8] = jnp.where(own_row == prior_last, 1.0, 0.0)
     sg[1, 8:16] = jnp.where(own_row == own_last, 1.0, 0.0)
     sum_up = jnp.where(t_at <= lane, 1.0, 0.0)
-    weights_1(1)
 
     def total_square(lx):
         s = sm[lx, 0, 16:24] + sm[lx, 1, 16:24] + sm[lx, 2, 16:24] + sm[lx, 3, 16:24]
@@ -391,7 +389,18 @@
                 ubuf.at[l + 1, pl.ds(T - 16, 16), :], halo.at[l], hs.at[l], hr.at[l], phase, seg + 1
             ).start()
 
-        weights_2(l + 1)
+        @pl.when(l == 0)
+        def _():
+            weights_1(1)
+
+        @pl.when(l > 0)
+        def _():
+            weights_2(l + 1)
+
+        @pl.when((l == 0) & (phase == 2))
+        def _():
+            send_weights()
+            send_params()
 
         @pl.when(phase != l)
         def _():
@@ -470,10 +479,14 @@
         def _():
             send_out(l)
 
+        @pl.when(l == 0)
+        def _():
+            weights_2(1)
+
         @pl.when(phase == l + 3)
         def _():
+            send_weights()
             send_params()
-            send_weights()
 
         cols = jnp.transpose(jnp.concatenate([run, cgain, jnp.zeros((T - 2 * PER, T), F32)], axis=0))
         for j in range(NCH):
@@ -691,7 +704,7 @@
             vmem((T, CH), BF16),
             vmem((GROUPS, 88, 128), F32),
             vmem((HEADS, 128), F32),
-            vmem((PROJ, MICRO * T), F32),
+            vmem((PROJ, T), F32),
             vmem((LAYERS, 88, 128), F32),
             vmem((8, T), jnp.int32),
             vmem((8, T), jnp.int32),

time: 200 us -> 197 us (0.985)
  Pallas kernels: 197 us -> 194 us
    pallas_call x1, Pallas kernels: 197 us -> 194 us  [body(): pl.pallas_call(functools.partial(kernel, nz), out_shape=jax.ShapeDtypeStr...]
where the time goes in v6:
time: 197 us
  Pallas kernels  194 us (98%)
  local copies, waits for them, and re-layouts  3.13 us (2%)
    pallas_call x1, Pallas kernels, body(): pl.pallas_call(functools.partial(kernel, nz), out_shape=jax.ShapeDtypeStr...  194 us

profile of v6, /device:TPU:249, one launch (start us, length us, event | category | flops | bytes accessed | tf_op | source)
XLA Modules:
  0.0 197.2 jit_solution(10393408587909466391)
XLA Ops:
  0.0 194.1 %shard_map.91 = bf16[1,2,128,4096]{3,2,1,0:T(8,128)(2,1)} custom-call(bf16[2,128,4096]{2,1,0:T(8,128)(2,1)} %stream_ref.1, s32[2,128]{1,0:T(2,128)} %ids_ref.1, bf16[1,576,4096]{2,1,0:T(8,128)(2,1)} %bitcast.1, f32[1,4,4096]{2,1,0:T(4,128)} %convw_ref.1, f32[1,4096]{1,0:T(1,128)} %convb_ref.1, f32[1,64]{1,0:T(1,128)} %decay_ref.1, f32[1,64]{1,0:T(1,128)} %stepb_ref.1, ...), custom_call_target="tpu_custom_call" | custom-call | tf_op jit(solution)/shard_map/pallas_call | solution.py:688
  194.1 3.1 %copy.11 = bf16[1,2,128,4096]{3,2,1,0:T(8,128)(2,1)} copy(bf16[1,2,128,4096]{3,2,1,0:T(8,128)(2,1)} %shard_map.91) | data formatting | bytes 4194304
